TPU v7x, 512 devices: a whole 4x8x8 slice. The times are simulated.
512 devices in a mesh: blk: 512 (over y, x, z, core).
Axes of the slice: x: 4, y: 8, z: 8, core: 2. Of those that a mesh axis runs over, the one named last changes fastest.
Arguments:
- concentration: float32 [1536, 4, 40, 1024], P('blk'), may hold values from 0.2 to 2
- potential_guess: float32 [1536, 40, 1024], P('blk'), may hold values from -3 to 3
- diffusivity: float32 [4], replicated, may hold values from 0.5 to 2
- block_rows: int32 [1536], P('blk'), may hold values from 20 to 40, as said below
- block_home: int32 [1536], replicated, may hold values from 0 to 1535, as said below
- face_match: int32 [1536, 2, 3], P('blk'), may hold values from -1 to 1535, as said below
Outputs:
- species_end: float32 [1536, 4, 40, 1024], P('blk')
- potential: float32 [1536, 40, 1024], P('blk')
Inputs may be any that keep to these rules, and one draw needn't show every extreme that they name: `block_rows`: the first block of every device has 40 live rows. `block_home`: A permutation of the block positions. `face_match`: matching is symmetric: a face's partner names it back with the same reverse flag, walls come in pairs of such faces. Every partner block lies on the same device as the face or on the device whose index is one higher or lower, cyclically over all devices; between two cyclically consecutive devices there is at most one matched (or wall-paired) face pair.
All inputs are finite; a program needn't handle non-finite values.
Results may differ from a plain program's by a relative error of at most 0.00002.
Values sent between devices are 32-bit elements; how exact they have to be, the bound alone decides.
No kernel may reach another device: no remote copies, remote signals or barrier semaphores. Data moves between devices by JAX's collectives and lax.ppermute only.
A program may use at most 128 MiB of HBM per device.

v0:
```python
import jax
import jax.numpy as jnp
from jax import lax
from jax.sharding import PartitionSpec as P

ROWS = 40
FACE = 1024
SWEEPS = 4


screening = 0.5
time_step = 0.1
smoother_weight = 0.8
coarse_weight = 0.8
valences = (1.0, -1.0, 2.0, -1.0)


def with_halo(x, sides, width):
    for axis, dim in sides:
        devices, length = (lax.axis_size(axis), x.shape[dim])
        up = [(i, (i + 1) % devices) for i in range(devices)]
        down = [(j, i) for i, j in up]
        last = lax.slice_in_dim(x, length - width, length, axis=dim)
        first = lax.slice_in_dim(x, 0, width, axis=dim)
        before = lax.ppermute(last, axis, up)
        after = lax.ppermute(first, axis, down)
        x = jnp.concatenate([before, x, after], axis=dim)
    return x


def face_rows_of(values, top_mask):
    south_side = values[:, :, 0, :]
    north_side = jnp.sum(values * top_mask[:, None, :, None], axis=2)
    return jnp.stack([south_side, north_side], axis=1)


def orient_ghosts(picked, face_match):
    reverse_flag = (face_match[:, :, 2] == 1)[:, :, None, None]
    flipped = jnp.where(reverse_flag, picked[..., ::-1], picked)
    is_open = (face_match[:, :, 0] >= 0)[:, :, None, None]
    return jnp.where(is_open, flipped, jnp.zeros_like(flipped))


def partner_position(face_match, block_home):
    partner_id = jnp.maximum(face_match[:, :, 0], 0)
    return block_home[partner_id]


def link_masks(block_rows, face_match):
    row_index = jnp.arange(ROWS, dtype=jnp.int32)[None, :]
    col_index = jnp.arange(FACE, dtype=jnp.int32)
    live_rows = block_rows[:, None]
    alive_mask = row_index < live_rows
    top_row = row_index == live_rows - 1
    south_open = (face_match[:, 0, 0] >= 0)[:, None]
    north_open = (face_match[:, 1, 0] >= 0)[:, None]
    up_link = alive_mask & ((row_index + 1 < live_rows) | top_row & north_open)
    down_link = alive_mask & ((row_index > 0) | south_open)
    up_link = up_link.astype(jnp.float32)[:, None, :, None]
    down_link = down_link.astype(jnp.float32)[:, None, :, None]
    left_link = (alive_mask[:, None, :, None] & (col_index > 0)[None, None, None, :]).astype(
        jnp.float32
    )
    right_link = (
        alive_mask[:, None, :, None] & (col_index < FACE - 1)[None, None, None, :]
    ).astype(jnp.float32)
    alive_float = alive_mask.astype(jnp.float32)[:, None, :, None]
    return (alive_float, top_row.astype(jnp.float32), (up_link, down_link, left_link, right_link))


def neighbor_values(values, ghosts, top_mask):
    zero_row = jnp.zeros_like(values[:, :, :1, :])
    first_row = (jnp.arange(ROWS, dtype=jnp.int32) == 0)[None, None, :, None]
    above_vals = jnp.concatenate([values[:, :, 1:, :], zero_row], axis=2)
    above_vals = jnp.where(top_mask[:, None, :, None] > 0, ghosts[:, 1][:, :, None, :], above_vals)
    below_vals = jnp.concatenate([zero_row, values[:, :, :-1, :]], axis=2)
    below_vals = jnp.where(first_row, ghosts[:, 0][:, :, None, :], below_vals)
    zero_col = jnp.zeros_like(values[..., :1])
    leftward = jnp.concatenate([zero_col, values[..., :-1]], axis=-1)
    rightward = jnp.concatenate([values[..., 1:], zero_col], axis=-1)
    return (above_vals, below_vals, leftward, rightward)


def apply_operator(values, neighbors, link_set):
    result = screening * values
    for link_mask, other in zip(link_set, neighbors):
        result = result + link_mask * (values - other)
    return result


def transport_rate(species, potential, species_nb, potential_nb, link_set, diffusivity):
    valence_col = jnp.array(valences, dtype=jnp.float32)[None, :, None, None]
    rate_sum = jnp.zeros_like(species)
    for link_mask, other, other_pot in zip(link_set, species_nb, potential_nb):
        rate_sum = rate_sum + link_mask * (
            other - species + valence_col * 0.5 * (species + other) * (other_pot - potential)
        )
    return diffusivity[None, :, None, None] * rate_sum


def body(concentration, potential_guess, diffusivity, block_rows, block_home, face_match):
    local_blocks = concentration.shape[0]
    devices = lax.axis_size("blk")
    own_index = lax.axis_index("blk")
    alive_float, top_mask, link_set = link_masks(block_rows, face_match)
    positions = partner_position(face_match, block_home)
    offset = (positions // local_blocks - own_index + 1) % devices
    face_index = offset * (2 * local_blocks) + positions % local_blocks * 2 + face_match[:, :, 1]
    coarse_index = offset * local_blocks + positions % local_blocks
    valence_col = jnp.array(valences, dtype=jnp.float32)[None, :, None, None]
    species_start = concentration * alive_float
    charge = jnp.sum(species_start * valence_col, axis=1, keepdims=True)
    guess = potential_guess[:, None] * alive_float
    diagonal = screening + link_set[0] + link_set[1] + link_set[2] + link_set[3]

    def ghosts_from(extended):
        flat_table = extended.reshape((-1,) + extended.shape[3:])
        return orient_ghosts(flat_table[face_index], face_match)

    def potential_ghosts(values):
        rows_out = face_rows_of(values, top_mask)
        extended = with_halo(rows_out[None], (("blk", 0),), 1)
        return ghosts_from(extended)

    def species_ghosts(values):
        rows_out = face_rows_of(values, top_mask)
        extended = with_halo(rows_out[None], (("blk", 0),), 1)
        return ghosts_from(extended)

    def smooth(values):
        neighbors = neighbor_values(values, potential_ghosts(values), top_mask)
        return (
            values
            + smoother_weight * (charge - apply_operator(values, neighbors, link_set)) / diagonal
        )

    smoothed = smooth(guess)
    residual = charge - apply_operator(
        smoothed, neighbor_values(smoothed, potential_ghosts(smoothed), top_mask), link_set
    )
    block_residual = jnp.sum(residual, axis=(1, 2, 3))
    open_south = (face_match[:, 0, 0] >= 0).astype(jnp.float32)
    open_north = (face_match[:, 1, 0] >= 0).astype(jnp.float32)
    coarse_diag = screening * (block_rows.astype(jnp.float32) * FACE) + FACE * (
        open_south + open_north
    )
    correction = jnp.zeros_like(block_residual)
    for step_index in range(SWEEPS):
        nearby = with_halo(correction[None], (("blk", 0),), 1).reshape(-1)
        neighbor_sum = (
            open_south * nearby[coarse_index[:, 0]] + open_north * nearby[coarse_index[:, 1]]
        )
        correction = (
            correction
            + coarse_weight
            * (block_residual - (coarse_diag * correction - FACE * neighbor_sum))
            / coarse_diag
        )
    corrected = smoothed + correction[:, None, None, None] * alive_float
    potential = smooth(corrected)
    potential_gh = potential_ghosts(potential)
    start_ghosts = species_ghosts(species_start)
    potential_nb = neighbor_values(potential, potential_gh, top_mask)
    start_nb = neighbor_values(species_start, start_ghosts, top_mask)
    species_mid = species_start + time_step * transport_rate(
        species_start, potential, start_nb, potential_nb, link_set, diffusivity
    )
    mid_nb = neighbor_values(species_mid, species_ghosts(species_mid), top_mask)
    mid_rate = transport_rate(species_mid, potential, mid_nb, potential_nb, link_set, diffusivity)
    species_end = 0.5 * species_start + 0.5 * (species_mid + time_step * mid_rate)
    return (species_end, potential[:, 0])


def solution(mesh):
    in_specs = (
        P("blk", None, None, None),
        P("blk", None, None),
        P(),
        P("blk"),
        P(),
        P("blk", None, None),
    )
    out_specs = (P("blk", None, None, None), P("blk", None, None))
    return jax.shard_map(body, mesh=mesh, in_specs=in_specs, out_specs=out_specs, check_vma=False)
```

profile of v0, /device:TPU:32, one launch (start us, length us, event | category | flops | bytes accessed | tf_op | source)
XLA Modules:
  0.0 204.3 jit_solution(9753422140418323826)
XLA Ops:
  1.2 12.5 %collective-permute-start.7 = (f32[1,3]{1,0:T(1,128)}, f32[1,3]{1,0:T(1,128)}, u32[]{:S(2)}, u32[]{:S(2)}) collective-permute-start(f32[1,3]{1,0:T(1,128)} %broadcast.629), channel_id=1, source_target_pairs={{1,0},{2,1},{3,2},{4,3},{5,4},{6,5},{7,6},{8,7},{9,8},{10,9},{11,1... | collective-permute-start | bytes 44 | tf_op jit(solution)/shard_map/ppermute | solution.py:26
  13.6 1.9 collective-permute-start.6
  17.2 1.3 fusion.37
  18.5 1.2 multiply_reduce_fusion.6
  19.8 9.1 %collective-permute-start.3 = (f32[1,3,2,1,1024]{4,2,1,3,0:T(2,128)S(1)}, f32[1,3,2,1,1024]{4,2,1,3,0:T(2,128)}, u32[]{:S(2)}, u32[]{:S(2)}) collective-permute-start(f32[1,3,2,1,1024]{4,2,1,3,0:T(2,128)S(1)} %bitcast.109), channel_id=1, source_target_pairs={{1,0},{2,1},{3,2},{4,3},{5,4},{6,5},{7,6},{8,7},{9,8},{10,9},{11,1... | collective-permute-start | bytes 73736 | tf_op jit(solution)/shard_map/ppermute | solution.py:26
  28.9 1.9 collective-permute-start.2
  30.8 2.3 %multiply_reduce_fusion.2 = (f32[3,4,1024]{2,1,0:T(4,128)S(1)}, f32[3,40,1024]{2,1,0:T(8,128)S(1)}, f32[3,4,40,1024]{3,2,1,0:T(8,128)S(1)}) fusion(f32[3,40]{1,0:T(4,128)S(1)} %get-tuple-element.69, f32[4]{0:T(128)} %constant.104.clone, f32[3,4,40,1024]{3,2,1,0:T(8,128)} %param.9, f32[3,40]{1,0:T(4,128)S(1)} %get-tuple-element.65), kind=kLoop, calls=%fused_computation.19 | loop fusion | flops 2322432 | bytes 4473808 | tf_op jit(solution)/shard_map/reduce_sum | solution.py:33
  34.0 9.1 %collective-permute-start.1 = (f32[1,3,2,4,1024]{4,2,3,1,0:T(2,128)}, f32[1,3,2,4,1024]{4,2,3,1,0:T(2,128)}, u32[]{:S(2)}, u32[]{:S(2)}) collective-permute-start(f32[1,3,2,4,1024]{4,2,3,1,0:T(2,128)} %maximum_bitcast_fusion), channel_id=1, source_target_pairs={{1,0},{2,1},{3,2},{4,3},{5,4},{6,5},{7,6},{8,7},{9,8},{10,9},{11,1... | collective-permute-start | bytes 294920 | tf_op jit(solution)/shard_map/ppermute | solution.py:26
  45.7 1.1 fusion.52
  47.9 2.7 %fusion.44 = (f32[3,4,40,1023]{3,2,1,0:T(8,128)}, f32[3,4,40,1023]{3,2,1,0:T(8,128)}) fusion(f32[3,4,40,1024]{3,2,1,0:T(8,128)S(1)} %get-tuple-element.16), kind=kLoop, calls=%fused_computation.166 | loop fusion | bytes 7856640 | tf_op jit(solution)/shard_map/slice | solution.py:79
  50.7 2.4 %fusion.43 = (f32[3,4,39,1024]{3,2,1,0:T(8,128)}, f32[3,4,39,1024]{3,2,1,0:T(8,128)}) fusion(f32[3,4,40,1024]{3,2,1,0:T(8,128)S(1)} %get-tuple-element.16), kind=kLoop, calls=%fused_computation.165 | loop fusion | bytes 7667712 | tf_op jit(solution)/shard_map/slice | solution.py:74
  54.8 1.9 collective-permute-start
  57.5 1.1 gather_fusion.5
  58.6 1.2 gather_fusion.4
  62.3 2.3 %multiply_reduce_fusion.5 = (f32[3,1024]{1,0:T(4,128)S(1)}, f32[3,1,40,1024]{3,2,0,1:T(8,128)S(1)}) fusion(f32[3,40]{1,0:T(4,128)S(1)} %get-tuple-element.69, f32[3,40]{1,0:T(4,128)} %add_add_fusion, f32[3,1,40,1023]{3,2,0,1:T(8,128)} %get-tuple-element.46, pred[1024]{0:T(1024)(128)(4,1)} %copy-done.22, f32[3,1,40,1023]{3,2,0,1:T(8,128)} %get-tuple-element.45, ...), kind=kLoop, calls=%fused_computation.55 | loop fusion | flops 3437568 | bytes 3456696 | tf_op jit(solution)/shard_map/reduce_sum | solution.py:33
  64.7 9.1 %collective-permute-start.5 = (f32[1,3,2,1,1024]{4,2,1,3,0:T(2,128)S(1)}, f32[1,3,2,1,1024]{4,2,1,3,0:T(2,128)S(1)}, u32[]{:S(2)}, u32[]{:S(2)}) collective-permute-start(f32[1,3,2,1,1024]{4,2,1,3,0:T(2,128)S(1)} %bitcast.115), channel_id=1, source_target_pairs={{1,0},{2,1},{3,2},{4,3},{5,4},{6,5},{7,6},{8,7},{9,8},{10,9},{11,1... | collective-permute-start | bytes 73736 | tf_op jit(solution)/shard_map/ppermute | solution.py:26
  73.7 1.9 collective-permute-start.4
  77.7 6.6 %collective-permute-done.4 = f32[1,3,2,1,1024]{4,2,1,3,0:T(2,128)S(1)} collective-permute-done((f32[1,3,2,1,1024]{4,2,1,3,0:T(2,128)S(1)}, f32[1,3,2,1,1024]{4,2,1,3,0:T(2,128)S(1)}, u32[]{:S(2)}, u32[]{:S(2)}) %collective-permute-start.4) | collective-permute-done | bytes 24608 | tf_op jit(solution)/shard_map/ppermute | solution.py:25
  85.9 1.3 gather_fusion.3
  89.6 2.0 fusion.11
  92.3 2.4 %collective-permute-start.9 = (f32[1,3]{1,0:T(1,128)S(1)}, f32[1,3]{1,0:T(1,128)S(1)}, u32[]{:S(2)}, u32[]{:S(2)}) collective-permute-start(f32[1,3]{1,0:T(1,128)S(1)} %bitcast.129), channel_id=1, source_target_pairs={{1,0},{2,1},{3,2},{4,3},{5,4},{6,5},{7,6},{8,7},{9,8},{10,9},{11,1... | collective-permute-start | bytes 44 | tf_op jit(solution)/shard_map/ppermute | solution.py:26
  94.8 1.9 collective-permute-start.8
  96.7 8.3 %collective-permute-done.8 = f32[1,3]{1,0:T(1,128)S(1)} collective-permute-done((f32[1,3]{1,0:T(1,128)S(1)}, f32[1,3]{1,0:T(1,128)S(1)}, u32[]{:S(2)}, u32[]{:S(2)}) %collective-permute-start.8) | collective-permute-done | bytes 44 | tf_op jit(solution)/shard_map/ppermute | solution.py:25
  106.7 1.9 collective-permute-start.11
  108.7 2.4 %collective-permute-start.10 = (f32[1,3]{1,0:T(1,128)S(1)}, f32[1,3]{1,0:T(1,128)S(1)}, u32[]{:S(2)}, u32[]{:S(2)}) collective-permute-start(f32[1,3]{1,0:T(1,128)S(1)} %bitcast.136), channel_id=1, source_target_pairs={{0,1},{1,2},{2,3},{3,4},{4,5},{5,6},{6,7},{7,8},{8,9},{9,10},{10,1... | collective-permute-start | bytes 44 | tf_op jit(solution)/shard_map/ppermute | solution.py:25
  111.1 7.9 %collective-permute-done.10 = f32[1,3]{1,0:T(1,128)S(1)} collective-permute-done((f32[1,3]{1,0:T(1,128)S(1)}, f32[1,3]{1,0:T(1,128)S(1)}, u32[]{:S(2)}, u32[]{:S(2)}) %collective-permute-start.10) | collective-permute-done | bytes 44 | tf_op jit(solution)/shard_map/ppermute | solution.py:25
  120.6 1.9 collective-permute-start.13
  122.5 2.4 %collective-permute-start.12 = (f32[1,3]{1,0:T(1,128)S(1)}, f32[1,3]{1,0:T(1,128)S(1)}, u32[]{:S(2)}, u32[]{:S(2)}) collective-permute-start(f32[1,3]{1,0:T(1,128)S(1)} %bitcast.133), channel_id=1, source_target_pairs={{0,1},{1,2},{2,3},{3,4},{4,5},{5,6},{6,7},{7,8},{8,9},{9,10},{10,1... | collective-permute-start | bytes 44 | tf_op jit(solution)/shard_map/ppermute | solution.py:25
  124.9 7.9 %collective-permute-done.12 = f32[1,3]{1,0:T(1,128)S(1)} collective-permute-done((f32[1,3]{1,0:T(1,128)S(1)}, f32[1,3]{1,0:T(1,128)S(1)}, u32[]{:S(2)}, u32[]{:S(2)}) %collective-permute-start.12) | collective-permute-done | bytes 44 | tf_op jit(solution)/shard_map/ppermute | solution.py:25
  134.8 1.9 collective-permute-start.15
  136.7 2.4 %collective-permute-start.14 = (f32[1,3,2,1,1024]{4,2,1,3,0:T(2,128)S(1)}, f32[1,3,2,1,1024]{4,2,1,3,0:T(2,128)S(1)}, u32[]{:S(2)}, u32[]{:S(2)}) collective-permute-start(f32[1,3,2,1,1024]{4,2,1,3,0:T(2,128)S(1)} %bitcast.119), channel_id=1, source_target_pairs={{0,1},{1,2},{2,3},{3,4},{4,5},{5,6},{6,7},{7,8},{8,9},{9,10},{10,1... | collective-permute-start | bytes 73736 | tf_op jit(solution)/shard_map/ppermute | solution.py:25
  141.4 5.9 %collective-permute-done.14 = f32[1,3,2,1,1024]{4,2,1,3,0:T(2,128)S(1)} collective-permute-done((f32[1,3,2,1,1024]{4,2,1,3,0:T(2,128)S(1)}, f32[1,3,2,1,1024]{4,2,1,3,0:T(2,128)S(1)}, u32[]{:S(2)}, u32[]{:S(2)}) %collective-permute-start.14) | collective-permute-done | bytes 24608 | tf_op jit(solution)/shard_map/ppermute | solution.py:25
  148.9 2.3 %multiply_reduce_fusion.3 = (f32[3,1024]{1,0:T(4,128)S(1)}, f32[3,1,40,1024]{3,2,0,1:T(8,128)S(1)}) fusion(f32[3,40]{1,0:T(4,128)S(1)} %get-tuple-element.69, f32[3,1,40,1024]{3,2,0,1:T(8,128)S(1)} %get-tuple-element.13, f32[3,40]{1,0:T(4,128)} %add_add_fusion, f32[3,1,40,1023]{3,2,0,1:T(8,128)} %get-tuple-element.38, pred[1024]{0:T(1024)(128)(4,1)S(1)} %copy-done.23, ...), kind=kLoop, calls=%fused_computation.53 | loop fusion | flops 3314688 | bytes 3456216 | tf_op jit(solution)/shard_map/reduce_sum | solution.py:33
  151.3 2.7 %collective-permute-start.17 = (f32[1,3,2,1,1024]{4,2,1,3,0:T(2,128)S(1)}, f32[1,3,2,1,1024]{4,2,1,3,0:T(2,128)S(1)}, u32[]{:S(2)}, u32[]{:S(2)}) collective-permute-start(f32[1,3,2,1,1024]{4,2,1,3,0:T(2,128)S(1)} %bitcast.112), channel_id=1, source_target_pairs={{1,0},{2,1},{3,2},{4,3},{5,4},{6,5},{7,6},{8,7},{9,8},{10,9},{11,1... | collective-permute-start | bytes 73736 | tf_op jit(solution)/shard_map/ppermute | solution.py:26
  154.0 1.9 collective-permute-start.16
  155.9 1.2 fusion.46
  158.2 1.1 pad_maximum_fusion
  161.0 3.5 %collective-permute-done.16 = f32[1,3,2,1,1024]{4,2,1,3,0:T(2,128)S(1)} collective-permute-done((f32[1,3,2,1,1024]{4,2,1,3,0:T(2,128)S(1)}, f32[1,3,2,1,1024]{4,2,1,3,0:T(2,128)S(1)}, u32[]{:S(2)}, u32[]{:S(2)}) %collective-permute-start.16) | collective-permute-done | bytes 24608 | tf_op jit(solution)/shard_map/ppermute | solution.py:25
  166.3 2.0 subtract_bitcast_fusion.3
  169.0 4.6 %multiply_reduce_fusion = (f32[3,4,1024]{2,1,0:T(4,128)S(1)}, f32[3,4,40,1024]{3,2,1,0:T(8,128)S(1)}) fusion(f32[3,40]{1,0:T(4,128)S(1)} %get-tuple-element.69, f32[3,4,40,1024]{3,2,1,0:T(8,128)S(1)} %get-tuple-element.16, f32[3,40,1024]{2,1,0:T(8,128)S(1)} %get-tuple-element.28, f32[3,4,40,1023]{3,2,1,0:T(8,128)S(1)} %copy-done.4, ...), kind=kLoop, calls=%fused_computation.16 | loop fusion | flops 16699392 | bytes 14792544 | tf_op jit(solution)/shard_map/reduce_sum | solution.py:33
  173.8 5.6 %collective-permute-start.19 = (f32[1,3,2,4,1024]{4,2,3,1,0:T(2,128)S(1)}, f32[1,3,2,4,1024]{4,2,3,1,0:T(2,128)S(1)}, u32[]{:S(2)}, u32[]{:S(2)}) collective-permute-start(f32[1,3,2,4,1024]{4,2,3,1,0:T(2,128)S(1)} %maximum_bitcast_fusion.1), channel_id=1, source_target_pairs={{1,0},{2,1},{3,2},{4,3},{5,4},{6,5},{7,6},{8,7},{9,8},{10,9},{11,1... | collective-permute-start | bytes 294920 | tf_op jit(solution)/shard_map/ppermute | solution.py:26
  179.4 2.1 %collective-permute-start.18 = (f32[1,3,2,4,1024]{4,2,3,1,0:T(2,128)S(1)}, f32[1,3,2,4,1024]{4,2,3,1,0:T(2,128)S(1)}, u32[]{:S(2)}, u32[]{:S(2)}) collective-permute-start(f32[1,3,2,4,1024]{4,2,3,1,0:T(2,128)S(1)} %maximum_bitcast_fusion.1), channel_id=1, source_target_pairs={{0,1},{1,2},{2,3},{3,4},{4,5},{5,6},{6,7},{7,8},{8,9},{9,10},{10,1... | collective-permute-start | bytes 294920 | tf_op jit(solution)/shard_map/ppermute | solution.py:25
  181.5 2.5 %fusion.41 = (f32[3,4,39,1024]{3,2,1,0:T(8,128)}, f32[3,4,39,1024]{3,2,1,0:T(8,128)}) fusion(f32[3,4,40,1024]{3,2,1,0:T(8,128)S(1)} %get-tuple-element.9), kind=kLoop, calls=%fused_computation.163 | loop fusion | bytes 7667712 | tf_op jit(solution)/shard_map/slice | solution.py:74
  184.0 2.8 %fusion.42 = (f32[3,4,40,1023]{3,2,1,0:T(8,128)}, f32[3,4,40,1023]{3,2,1,0:T(8,128)}) fusion(f32[3,4,40,1024]{3,2,1,0:T(8,128)S(1)} %get-tuple-element.9), kind=kLoop, calls=%fused_computation.164 | loop fusion | bytes 7856640 | tf_op jit(solution)/shard_map/slice | solution.py:79
  186.7 4.0 %collective-permute-done.18 = f32[1,3,2,4,1024]{4,2,3,1,0:T(2,128)S(1)} collective-permute-done((f32[1,3,2,4,1024]{4,2,3,1,0:T(2,128)S(1)}, f32[1,3,2,4,1024]{4,2,3,1,0:T(2,128)S(1)}, u32[]{:S(2)}, u32[]{:S(2)}) %collective-permute-start.18) | collective-permute-done | bytes 98336 | tf_op jit(solution)/shard_map/ppermute | solution.py:25
  191.8 1.7 gather_fusion.14
  193.5 2.9 %rev.23 = f32[3,2,4,1024]{3,2,1,0:T(4,128)} reverse(f32[3,2,4,1024]{3,2,1,0:T(4,128)S(1)} %bitcast.103), dimensions={3} | reverse | bytes 196608 | tf_op jit(solution)/shard_map/rev | solution.py:39
  197.4 7.0 %add_multiply_fusion = f32[3,4,40,1024]{3,2,1,0:T(8,128)} fusion(f32[3,4,40,1024]{3,2,1,0:T(8,128)S(1)} %get-tuple-element.16, f32[3,4,40,1024]{3,2,1,0:T(8,128)} %copy-done.1, f32[3,4,40,1023]{3,2,1,0:T(8,128)} %get-tuple-element.20, f32[3,4,40,1023]{3,2,1,0:T(8,128)} %get-tuple-element.19, f32[3,4,39,1024]{3,2,1,0:T(8,128)} %get-tuple-element.18, ...), kind=kLoop, calls=%fused_computation.15 | loop fusion | flops 16711680 | bytes 16708992 | tf_op jit(solution)/shard_map/add | solution.py:170
  (227 shorter events, 34.4 us)
Async XLA Ops:
  0.6 43.9 %copy-start = (s32[1536]{0:T(1024)S(1)}, s32[1536]{0:T(1024)}, u32[]{:S(2)}) copy-start(s32[1536]{0:T(1024)} %param.13) | copy-start | bytes 18436
  1.2 53.7 %collective-permute-start.7 = (f32[1,3]{1,0:T(1,128)}, f32[1,3]{1,0:T(1,128)}, u32[]{:S(2)}, u32[]{:S(2)}) collective-permute-start(f32[1,3]{1,0:T(1,128)} %broadcast.629), channel_id=1, source_target_pairs={{1,0},{2,1},{3,2},{4,3},{5,4},{6,5},{7,6},{8,7},{9,8},{10,9},{11,1... | collective-permute-start | bytes 44 | tf_op jit(solution)/shard_map/ppermute | solution.py:26
  13.6 43.1 %collective-permute-start.6 = (f32[1,3]{1,0:T(1,128)}, f32[1,3]{1,0:T(1,128)}, u32[]{:S(2)}, u32[]{:S(2)}) collective-permute-start(f32[1,3]{1,0:T(1,128)} %broadcast.629), channel_id=1, source_target_pairs={{0,1},{1,2},{2,3},{3,4},{4,5},{5,6},{6,7},{7,8},{8,9},{9,10},{10,1... | collective-permute-start | bytes 44 | tf_op jit(solution)/shard_map/ppermute | solution.py:25
  17.2 26.4 %copy-start.35 = (pred[3]{0:T(512)(128)(4,1)}, pred[3]{0:T(512)(128)(4,1)S(1)}, u32[]{:S(2)}) copy-start(pred[3]{0:T(512)(128)(4,1)S(1)} %get-tuple-element.4) | copy-start | bytes 13
  17.2 26.4 %copy-start.37 = (pred[3]{0:T(512)(128)(4,1)}, pred[3]{0:T(512)(128)(4,1)S(1)}, u32[]{:S(2)}) copy-start(pred[3]{0:T(512)(128)(4,1)S(1)} %get-tuple-element.5) | copy-start | bytes 13
  18.5 14.6 %copy-start.21 = (f32[3,40]{1,0:T(4,128)}, f32[3,40]{1,0:T(4,128)S(1)}, u32[]{:S(2)}) copy-start(f32[3,40]{1,0:T(4,128)S(1)} %get-tuple-element.65) | copy-start | bytes 1444
  18.5 43.7 %copy-start.13 = (f32[3,40]{1,0:T(4,128)}, f32[3,40]{1,0:T(4,128)S(1)}, u32[]{:S(2)}) copy-start(f32[3,40]{1,0:T(4,128)S(1)} %get-tuple-element.66) | copy-start | bytes 1444
  19.8 23.8 %copy-start.33 = (s32[3]{0:T(128)S(1)}, s32[3]{0:T(128)}, u32[]{:S(2)}) copy-start(s32[3]{0:T(128)} %param.12) | copy-start | bytes 40
  19.8 24.4 %copy-start.20 = (s32[3,2,3]{2,1,0:T(2,128)S(1)}, s32[3,2,3]{2,1,0:T(2,128)}, u32[]{:S(2)}) copy-start(s32[3,2,3]{2,1,0:T(2,128)} %param.14) | copy-start | bytes 220
  19.8 40.0 %collective-permute-start.3 = (f32[1,3,2,1,1024]{4,2,1,3,0:T(2,128)S(1)}, f32[1,3,2,1,1024]{4,2,1,3,0:T(2,128)}, u32[]{:S(2)}, u32[]{:S(2)}) collective-permute-start(f32[1,3,2,1,1024]{4,2,1,3,0:T(2,128)S(1)} %bitcast.109), channel_id=1, source_target_pairs={{1,0},{2,1},{3,2},{4,3},{5,4},{6,5},{7,6},{8,7},{9,8},{10,9},{11,1... | collective-permute-start | bytes 73736 | tf_op jit(solution)/shard_map/ppermute | solution.py:26
  28.9 30.9 %collective-permute-start.2 = (f32[1,3,2,1,1024]{4,2,1,3,0:T(2,128)S(1)}, f32[1,3,2,1,1024]{4,2,1,3,0:T(2,128)}, u32[]{:S(2)}, u32[]{:S(2)}) collective-permute-start(f32[1,3,2,1,1024]{4,2,1,3,0:T(2,128)S(1)} %bitcast.110), channel_id=1, source_target_pairs={{0,1},{1,2},{2,3},{3,4},{4,5},{5,6},{6,7},{7,8},{8,9},{9,10},{10,1... | collective-permute-start | bytes 73736 | tf_op jit(solution)/shard_map/ppermute | solution.py:25
  34.0 124.3 %collective-permute-start.1 = (f32[1,3,2,4,1024]{4,2,3,1,0:T(2,128)}, f32[1,3,2,4,1024]{4,2,3,1,0:T(2,128)}, u32[]{:S(2)}, u32[]{:S(2)}) collective-permute-start(f32[1,3,2,4,1024]{4,2,3,1,0:T(2,128)} %maximum_bitcast_fusion), channel_id=1, source_target_pairs={{1,0},{2,1},{3,2},{4,3},{5,4},{6,5},{7,6},{8,7},{9,8},{10,9},{11,1... | collective-permute-start | bytes 294920 | tf_op jit(solution)/shard_map/ppermute | solution.py:26
  44.2 9.4 %copy-start.22 = (pred[1024]{0:T(1024)(128)(4,1)}, pred[1024]{0:T(1024)(128)(4,1)S(1)}, u32[]{:S(2)}) copy-start(pred[1024]{0:T(1024)(128)(4,1)S(1)} %get-tuple-element.74) | copy-start | bytes 3076
  44.3 9.5 %copy-start.24 = (pred[1024]{0:T(1024)(128)(4,1)}, pred[1024]{0:T(1024)(128)(4,1)S(1)}, u32[]{:S(2)}) copy-start(pred[1024]{0:T(1024)(128)(4,1)S(1)} %get-tuple-element.75) | copy-start | bytes 3076
  53.1 9.2 %copy-start.12 = (f32[3,40,1024]{2,1,0:T(8,128)S(1)}, f32[3,40,1024]{2,1,0:T(8,128)}, u32[]{:S(2)}) copy-start(f32[3,40,1024]{2,1,0:T(8,128)} %param.10) | copy-start | bytes 1474564
  53.2 9.0 %copy-start.27 = (pred[3,2]{1,0:T(4,128)(4,1)}, pred[3,2]{1,0:T(4,128)(4,1)S(1)}, u32[]{:S(2)}) copy-start(pred[3,2]{1,0:T(4,128)(4,1)S(1)} %get-tuple-element.72) | copy-start | bytes 22
  53.2 9.0 %copy-start.30 = (pred[3,2]{1,0:T(4,128)(4,1)}, pred[3,2]{1,0:T(4,128)(4,1)S(1)}, u32[]{:S(2)}) copy-start(pred[3,2]{1,0:T(4,128)(4,1)S(1)} %get-tuple-element.73) | copy-start | bytes 22
  53.6 7.6 %copy-start.17 = (s32[1024]{0:T(1024)}, s32[1024]{0:T(1024)S(1)}, u32[]{:S(2)}) copy-start(s32[1024]{0:T(1024)S(1)} %pad_clamp_fusion.2) | copy-start | bytes 12292
  53.7 7.6 %copy-start.41 = (s32[1024]{0:T(1024)}, s32[1024]{0:T(1024)S(1)}, u32[]{:S(2)}) copy-start(s32[1024]{0:T(1024)S(1)} %get-tuple-element.77) | copy-start | bytes 12292
  53.7 7.6 %copy-start.42 = (s32[1024]{0:T(1024)}, s32[1024]{0:T(1024)S(1)}, u32[]{:S(2)}) copy-start(s32[1024]{0:T(1024)S(1)} %get-tuple-element.76) | copy-start | bytes 12292
  54.8 103.4 %collective-permute-start = (f32[1,3,2,4,1024]{4,2,3,1,0:T(2,128)}, f32[1,3,2,4,1024]{4,2,3,1,0:T(2,128)}, u32[]{:S(2)}, u32[]{:S(2)}) collective-permute-start(f32[1,3,2,4,1024]{4,2,3,1,0:T(2,128)} %maximum_bitcast_fusion), channel_id=1, source_target_pairs={{0,1},{1,2},{2,3},{3,4},{4,5},{5,6},{6,7},{7,8},{8,9},{9,10},{10,1... | collective-permute-start | bytes 294920 | tf_op jit(solution)/shard_map/ppermute | solution.py:25
  64.7 13.0 %collective-permute-start.5 = (f32[1,3,2,1,1024]{4,2,1,3,0:T(2,128)S(1)}, f32[1,3,2,1,1024]{4,2,1,3,0:T(2,128)S(1)}, u32[]{:S(2)}, u32[]{:S(2)}) collective-permute-start(f32[1,3,2,1,1024]{4,2,1,3,0:T(2,128)S(1)} %bitcast.115), channel_id=1, source_target_pairs={{1,0},{2,1},{3,2},{4,3},{5,4},{6,5},{7,6},{8,7},{9,8},{10,9},{11,1... | collective-permute-start | bytes 73736 | tf_op jit(solution)/shard_map/ppermute | solution.py:26
  73.7 10.6 %collective-permute-start.4 = (f32[1,3,2,1,1024]{4,2,1,3,0:T(2,128)S(1)}, f32[1,3,2,1,1024]{4,2,1,3,0:T(2,128)S(1)}, u32[]{:S(2)}, u32[]{:S(2)}) collective-permute-start(f32[1,3,2,1,1024]{4,2,1,3,0:T(2,128)S(1)} %bitcast.116), channel_id=1, source_target_pairs={{0,1},{1,2},{2,3},{3,4},{4,5},{5,6},{6,7},{7,8},{8,9},{9,10},{10,1... | collective-permute-start | bytes 73736 | tf_op jit(solution)/shard_map/ppermute | solution.py:25
  89.5 17.2 %copy-start.34 = (s32[3]{0:T(128)S(1)}, s32[3]{0:T(128)}, u32[]{:S(2)}) copy-start(s32[3]{0:T(128)} %param.12) | copy-start | bytes 40
  89.5 17.2 %copy-start.36 = (pred[3]{0:T(512)(128)(4,1)S(1)}, pred[3]{0:T(512)(128)(4,1)}, u32[]{:S(2)}) copy-start(pred[3]{0:T(512)(128)(4,1)} %copy-done.35) | copy-start | bytes 13
  89.5 17.1 %copy-start.38 = (pred[3]{0:T(512)(128)(4,1)S(1)}, pred[3]{0:T(512)(128)(4,1)}, u32[]{:S(2)}) copy-start(pred[3]{0:T(512)(128)(4,1)} %copy-done.37) | copy-start | bytes 13
  92.3 4.4 %collective-permute-start.9 = (f32[1,3]{1,0:T(1,128)S(1)}, f32[1,3]{1,0:T(1,128)S(1)}, u32[]{:S(2)}, u32[]{:S(2)}) collective-permute-start(f32[1,3]{1,0:T(1,128)S(1)} %bitcast.129), channel_id=1, source_target_pairs={{1,0},{2,1},{3,2},{4,3},{5,4},{6,5},{7,6},{8,7},{9,8},{10,9},{11,1... | collective-permute-start | bytes 44 | tf_op jit(solution)/shard_map/ppermute | solution.py:26
  94.8 10.3 %collective-permute-start.8 = (f32[1,3]{1,0:T(1,128)S(1)}, f32[1,3]{1,0:T(1,128)S(1)}, u32[]{:S(2)}, u32[]{:S(2)}) collective-permute-start(f32[1,3]{1,0:T(1,128)S(1)} %bitcast.130), channel_id=1, source_target_pairs={{0,1},{1,2},{2,3},{3,4},{4,5},{5,6},{6,7},{7,8},{8,9},{9,10},{10,1... | collective-permute-start | bytes 44 | tf_op jit(solution)/shard_map/ppermute | solution.py:25
  106.7 4.3 %collective-permute-start.11 = (f32[1,3]{1,0:T(1,128)S(1)}, f32[1,3]{1,0:T(1,128)S(1)}, u32[]{:S(2)}, u32[]{:S(2)}) collective-permute-start(f32[1,3]{1,0:T(1,128)S(1)} %bitcast.135), channel_id=1, source_target_pairs={{1,0},{2,1},{3,2},{4,3},{5,4},{6,5},{7,6},{8,7},{9,8},{10,9},{11,1... | collective-permute-start | bytes 44 | tf_op jit(solution)/shard_map/ppermute | solution.py:26
  108.7 10.3 %collective-permute-start.10 = (f32[1,3]{1,0:T(1,128)S(1)}, f32[1,3]{1,0:T(1,128)S(1)}, u32[]{:S(2)}, u32[]{:S(2)}) collective-permute-start(f32[1,3]{1,0:T(1,128)S(1)} %bitcast.136), channel_id=1, source_target_pairs={{0,1},{1,2},{2,3},{3,4},{4,5},{5,6},{6,7},{7,8},{8,9},{9,10},{10,1... | collective-permute-start | bytes 44 | tf_op jit(solution)/shard_map/ppermute | solution.py:25
  120.6 4.3 %collective-permute-start.13 = (f32[1,3]{1,0:T(1,128)S(1)}, f32[1,3]{1,0:T(1,128)S(1)}, u32[]{:S(2)}, u32[]{:S(2)}) collective-permute-start(f32[1,3]{1,0:T(1,128)S(1)} %bitcast.132), channel_id=1, source_target_pairs={{1,0},{2,1},{3,2},{4,3},{5,4},{6,5},{7,6},{8,7},{9,8},{10,9},{11,1... | collective-permute-start | bytes 44 | tf_op jit(solution)/shard_map/ppermute | solution.py:26
  122.5 10.3 %collective-permute-start.12 = (f32[1,3]{1,0:T(1,128)S(1)}, f32[1,3]{1,0:T(1,128)S(1)}, u32[]{:S(2)}, u32[]{:S(2)}) collective-permute-start(f32[1,3]{1,0:T(1,128)S(1)} %bitcast.133), channel_id=1, source_target_pairs={{0,1},{1,2},{2,3},{3,4},{4,5},{5,6},{6,7},{7,8},{8,9},{9,10},{10,1... | collective-permute-start | bytes 44 | tf_op jit(solution)/shard_map/ppermute | solution.py:25
  134.8 12.7 %copy-start.18 = (s32[1024]{0:T(1024)S(1)}, s32[1024]{0:T(1024)}, u32[]{:S(2)}) copy-start(s32[1024]{0:T(1024)} %copy-done.17) | copy-start | bytes 12292
  134.8 14.0 %copy-start.28 = (pred[3,2]{1,0:T(4,128)(4,1)S(1)}, pred[3,2]{1,0:T(4,128)(4,1)}, u32[]{:S(2)}) copy-start(pred[3,2]{1,0:T(4,128)(4,1)} %copy-done.27) | copy-start | bytes 22
  134.8 14.0 %copy-start.31 = (pred[3,2]{1,0:T(4,128)(4,1)S(1)}, pred[3,2]{1,0:T(4,128)(4,1)}, u32[]{:S(2)}) copy-start(pred[3,2]{1,0:T(4,128)(4,1)} %copy-done.30) | copy-start | bytes 22
  134.8 14.1 %copy-start.14 = (f32[3,40]{1,0:T(4,128)S(1)}, f32[3,40]{1,0:T(4,128)}, u32[]{:S(2)}) copy-start(f32[3,40]{1,0:T(4,128)} %copy-done.13) | copy-start | bytes 1444
  134.8 14.1 %copy-start.23 = (pred[1024]{0:T(1024)(128)(4,1)S(1)}, pred[1024]{0:T(1024)(128)(4,1)}, u32[]{:S(2)}) copy-start(pred[1024]{0:T(1024)(128)(4,1)} %copy-done.22) | copy-start | bytes 3076
  134.8 14.1 %copy-start.25 = (pred[1024]{0:T(1024)(128)(4,1)S(1)}, pred[1024]{0:T(1024)(128)(4,1)}, u32[]{:S(2)}) copy-start(pred[1024]{0:T(1024)(128)(4,1)} %copy-done.24) | copy-start | bytes 3076
  134.8 6.6 %collective-permute-start.15 = (f32[1,3,2,1,1024]{4,2,1,3,0:T(2,128)S(1)}, f32[1,3,2,1,1024]{4,2,1,3,0:T(2,128)S(1)}, u32[]{:S(2)}, u32[]{:S(2)}) collective-permute-start(f32[1,3,2,1,1024]{4,2,1,3,0:T(2,128)S(1)} %bitcast.118), channel_id=1, source_target_pairs={{1,0},{2,1},{3,2},{4,3},{5,4},{6,5},{7,6},{8,7},{9,8},{10,9},{11,1... | collective-permute-start | bytes 73736 | tf_op jit(solution)/shard_map/ppermute | solution.py:26
  136.7 10.6 %collective-permute-start.14 = (f32[1,3,2,1,1024]{4,2,1,3,0:T(2,128)S(1)}, f32[1,3,2,1,1024]{4,2,1,3,0:T(2,128)S(1)}, u32[]{:S(2)}, u32[]{:S(2)}) collective-permute-start(f32[1,3,2,1,1024]{4,2,1,3,0:T(2,128)S(1)} %bitcast.119), channel_id=1, source_target_pairs={{0,1},{1,2},{2,3},{3,4},{4,5},{5,6},{6,7},{7,8},{8,9},{9,10},{10,1... | collective-permute-start | bytes 73736 | tf_op jit(solution)/shard_map/ppermute | solution.py:25
  151.2 14.9 %copy-start.2 = (f32[3,1,40,1024]{3,2,0,1:T(8,128)}, f32[3,1,40,1024]{3,2,0,1:T(8,128)S(1)}, u32[]{:S(2)}) copy-start(f32[3,1,40,1024]{3,2,0,1:T(8,128)S(1)} %get-tuple-element.11) | copy-start | bytes 1474564
  151.3 9.7 %collective-permute-start.17 = (f32[1,3,2,1,1024]{4,2,1,3,0:T(2,128)S(1)}, f32[1,3,2,1,1024]{4,2,1,3,0:T(2,128)S(1)}, u32[]{:S(2)}, u32[]{:S(2)}) collective-permute-start(f32[1,3,2,1,1024]{4,2,1,3,0:T(2,128)S(1)} %bitcast.112), channel_id=1, source_target_pairs={{1,0},{2,1},{3,2},{4,3},{5,4},{6,5},{7,6},{8,7},{9,8},{10,9},{11,1... | collective-permute-start | bytes 73736 | tf_op jit(solution)/shard_map/ppermute | solution.py:26
  154.0 10.6 %collective-permute-start.16 = (f32[1,3,2,1,1024]{4,2,1,3,0:T(2,128)S(1)}, f32[1,3,2,1,1024]{4,2,1,3,0:T(2,128)S(1)}, u32[]{:S(2)}, u32[]{:S(2)}) collective-permute-start(f32[1,3,2,1,1024]{4,2,1,3,0:T(2,128)S(1)} %bitcast.113), channel_id=1, source_target_pairs={{0,1},{1,2},{2,3},{3,4},{4,5},{5,6},{6,7},{7,8},{8,9},{9,10},{10,1... | collective-permute-start | bytes 73736 | tf_op jit(solution)/shard_map/ppermute | solution.py:25
  173.7 10.3 %copy-start.1 = (f32[3,4,40,1024]{3,2,1,0:T(8,128)}, f32[3,4,40,1024]{3,2,1,0:T(8,128)S(1)}, u32[]{:S(2)}) copy-start(f32[3,4,40,1024]{3,2,1,0:T(8,128)S(1)} %get-tuple-element.9) | copy-start | bytes 5898244
  173.8 12.9 %collective-permute-start.19 = (f32[1,3,2,4,1024]{4,2,3,1,0:T(2,128)S(1)}, f32[1,3,2,4,1024]{4,2,3,1,0:T(2,128)S(1)}, u32[]{:S(2)}, u32[]{:S(2)}) collective-permute-start(f32[1,3,2,4,1024]{4,2,3,1,0:T(2,128)S(1)} %maximum_bitcast_fusion.1), channel_id=1, source_target_pairs={{1,0},{2,1},{3,2},{4,3},{5,4},{6,5},{7,6},{8,7},{9,8},{10,9},{11,1... | collective-permute-start | bytes 294920 | tf_op jit(solution)/shard_map/ppermute | solution.py:26
  179.4 11.4 %collective-permute-start.18 = (f32[1,3,2,4,1024]{4,2,3,1,0:T(2,128)S(1)}, f32[1,3,2,4,1024]{4,2,3,1,0:T(2,128)S(1)}, u32[]{:S(2)}, u32[]{:S(2)}) collective-permute-start(f32[1,3,2,4,1024]{4,2,3,1,0:T(2,128)S(1)} %maximum_bitcast_fusion.1), channel_id=1, source_target_pairs={{0,1},{1,2},{2,3},{3,4},{4,5},{5,6},{6,7},{7,8},{8,9},{9,10},{10,1... | collective-permute-start | bytes 294920 | tf_op jit(solution)/shard_map/ppermute | solution.py:25
  186.7 10.6 %copy-start.8 = (f32[3,40,1024]{2,1,0:T(8,128)S(1)}, f32[3,40,1024]{2,1,0:T(8,128)}, u32[]{:S(2)}) copy-start(f32[3,40,1024]{2,1,0:T(8,128)} %copy-done.7) | copy-start | bytes 1474564
  186.7 10.6 %copy-start.16 = (f32[3,40]{1,0:T(4,128)S(1)}, f32[3,40]{1,0:T(4,128)}, u32[]{:S(2)}) copy-start(f32[3,40]{1,0:T(4,128)} %copy-done.13) | copy-start | bytes 1444
  (17 other events, 64.6 us)
where the time goes:
time: 206 us; the launch traced here: 204 us
  starting transfers between devices  76.9 us (37%)
  local copies, waits for them, and re-layouts  44.6 us (22%)
  waiting for transfers between devices  44.3 us (22%)
  other arithmetic  36.7 us (18%)
    ppermute x10, starting transfers between devices, with_halo(): after = lax.ppermute(first, axis, down)  56.1 us
    ppermute x10, waiting for transfers between devices, with_halo(): before = lax.ppermute(last, axis, up)  44.2 us
    ppermute x10, starting transfers between devices, with_halo(): before = lax.ppermute(last, axis, up)  20.8 us
    reduce_sum x6, other arithmetic, face_rows_of(): north_side = jnp.sum(values * top_mask[:, None, :, None], axis=2)  12.8 us
    slice x6, local copies, waits for them, and re-layouts, neighbor_values(): leftward = jnp.concatenate([zero_col, values[..., :-1]], axis=-1)  10 us
    slice x6, local copies, waits for them, and re-layouts, neighbor_values(): above_vals = jnp.concatenate([values[:, :, 1:, :], zero_row], axis=2)  9.08 us
    add x1, other arithmetic, body(): 0.5 * species_start + 0.5 * (species_mid + time_step * mid_rate)  6.96 us
    rev x6, local copies, waits for them, and re-layouts, orient_ghosts(): flipped = jnp.where(reverse_flag, picked[..., ::-1], picked)  6.63 us
  transfers between devices with their start and end apart: 20, of which 7 were waited for; matrix products, arithmetic and copies ran while one was open for 28% of the time, Pallas kernels for 0%

commit v1 on v0

v1 whole, which is shorter than its diff:
```python
import functools

import jax
import jax.numpy as jnp
from jax import lax
from jax.experimental import pallas as pl
from jax.experimental.pallas import tpu as pltpu
from jax.sharding import PartitionSpec as P

AXIS = "blk"
B, S, ROWS, FACE = 3, 4, 40, 1024
NT = FACE // 128
LO = 8
H = 56
NI = 6
VALENCES = (1.0, -1.0, 2.0, -1.0)
W_IN, W_EDGE = 0.8 / 4.5, 0.8 / 3.5
WALL = -1000.0
MID = 18
F32 = jnp.float32


def face_info(match_s, home_s, b, side, me, devices):
    g = match_s[b, side, 0]
    pos = home_s[jnp.maximum(g, 0)]
    dev = lax.div(pos, jnp.int32(B))
    pb = pos - dev * B
    off = lax.rem(dev - me + 1 + devices, devices)
    return g >= 0, off, pb, match_s[b, side, 1], match_s[b, side, 2], (off - 1) * B + pb - b


def iota(shape, dim):
    return lax.broadcasted_iota(jnp.int32, shape, dim)


def pack_kernel(devices, conc, pot, rows_s, home_s, match_s, strips, msg_e, msg_o, U, G, Q, sem):
    me = lax.axis_index(AXIS)
    core = lax.rem(me, 2)

    def copies(b):
        out = []
        for j in range(NT):
            cols = pl.ds(128 * j, 128)
            out.append(pltpu.make_async_copy(conc.at[b, :, :, cols], U.at[b, :, j, pl.ds(LO, ROWS), :], sem.at[b]))
            out.append(pltpu.make_async_copy(pot.at[b, :, cols], G.at[b, j, pl.ds(LO, ROWS), :], sem.at[b]))
        return out

    for b in range(B):
        for c in copies(b):
            c.start()

    rowid = iota((ROWS, 128), 0)
    lane = iota((ROWS, 128), 1)
    first, last = lane == 0, lane == 127
    zero = jnp.zeros((ROWS, 128), F32)
    l8, s8 = iota((8, 128), 1), iota((8, 128), 0)
    mirror = 127 - l8

    def block(b, carry):
        W, fe, fo = carry
        for c in copies(b):
            c.wait()
        n = rows_s[b]
        info = [face_info(match_s, home_s, b, side, me, devices) for side in range(2)]
        live = rowid < n
        pad = jnp.zeros((8, 128), F32)
        for j in range(NT):
            c = [U[b, s, j, LO : LO + ROWS, :] for s in range(S)]
            q = c[0] - c[1] + 2.0 * c[2] - c[3]
            Q[b, j, LO : LO + ROWS, :] = jnp.where(live, q, 0.0)
            G[b, j, LO : LO + ROWS, :] = jnp.where(live, G[b, j, LO : LO + ROWS, :], 0.0)
            G[b, j, 0:LO, :] = pad
            G[b, j, LO + ROWS : H, :] = pad
        op = [i[0].astype(F32) for i in info]
        links = (
            2.0
            - jnp.where(rowid == 0, 1.0 - op[0], 0.0)
            - jnp.where(rowid == n - 1, 1.0 - op[1], 0.0)
        )
        w_in = jnp.where(live, 0.8 / (2.5 + links), 0.0)
        w_edge = jnp.where(live, 0.8 / (1.5 + links), 0.0)
        g = [G[b, j, LO : LO + ROWS, :] for j in range(NT)]
        gr = [pltpu.roll(x, 1, 1) for x in g]
        gl = [pltpu.roll(x, 127, 1) for x in g]
        total = s_sum = t_sum = zero
        for j in range(NT):
            left = jnp.where(first, gr[j - 1] if j else zero, gr[j])
            right = jnp.where(last, gl[j + 1] if j < NT - 1 else zero, gl[j])
            near = (
                G[b, j, LO + 1 : LO + 1 + ROWS, :] + G[b, j, LO - 1 : LO - 1 + ROWS, :] + left + right
            )
            w, wf = w_in, W_IN
            if j in (0, NT - 1):
                edge = first if j == 0 else last
                w, wf = jnp.where(edge, w_edge, w_in), jnp.where(edge, W_EDGE, W_IN)
            q = Q[b, j, LO : LO + ROWS, :]
            sm = 0.2 * g[j] + w * (q + near)
            total += q - 0.5 * sm
            s_sum += sm
            t_sum += wf * g[j]
        own = t_sum - s_sum
        away = s_sum - 1.5 * t_sum
        ends = [rowid == 0, rowid == n - 1]
        total += jnp.where(ends[0], op[0] * own, 0.0) + jnp.where(ends[1], op[1] * own, 0.0)
        vals = [jnp.sum(total, keepdims=True)]
        vals.append(1.0 / jnp.full((1, 1), 512.0 * n.astype(F32) + 1024.0 * (op[0] + op[1]), F32))
        vals += [jnp.sum(jnp.where(e, away, 0.0), keepdims=True) for e in ends]
        vals += [
            jnp.full((1, 1), jnp.where(i[0], i[5].astype(F32), WALL), F32) for i in info
        ]
        col = jnp.zeros((8, 128), F32)
        for k, v in enumerate(vals):
            col = jnp.where(s8 == k, v, col)
        W = jnp.where(l8 == MID + B * core + b, col, W)
        for side in range(2):
            f = 2 * b + side
            is_open, off, _, _, rev, _ = info[side]
            even = is_open & (off == 2 - 2 * core)
            odd = is_open & (off == 2 * core)
            fe, fo = jnp.where(even, f, fe), jnp.where(odd, f, fo)
            for k in range(4):
                row = LO + k if side == 0 else LO + n - 1 - k
                at = pl.ds(row, 1)
                strips[f, :, k : k + 1, :] = G[b, :, at, :]
                if k < 3:
                    strips[f, :, 4 + k : 5 + k, :] = Q[b, :, at, :]
                if k < 2:
                    for s in range(S):
                        strips[f, :, 7 + 2 * s + k : 8 + 2 * s + k, :] = U[b, s, :, at, :]

            @pl.when(rev == 1)
            def _():
                for j in range(NT // 2):
                    for h in range(0, 16, 8):
                        x = strips[f, j, h : h + 8, :]
                        y = strips[f, NT - 1 - j, h : h + 8, :]
                        strips[f, j, h : h + 8, :] = jnp.take_along_axis(y, mirror, axis=1)
                        strips[f, NT - 1 - j, h : h + 8, :] = jnp.take_along_axis(x, mirror, axis=1)

        return W, fe, fo

    for f in range(2 * B):
        strips[f, :, 15:16, :] = jnp.zeros((NT, 1, 128), F32)
    W, fe, fo = lax.fori_loop(
        0, B, block, (jnp.zeros((8, 128), F32), jnp.int32(0), jnp.int32(0))
    )
    for msg, f in ((msg_e, fe), (msg_o, fo)):
        for j in range(NT):
            msg[j] = strips[f, j]
        msg[NT, 0:8, :] = W
        msg[NT, 8:16, :] = jnp.zeros((8, 128), F32)


def turn(x, shift, core):
    return jnp.where(core == 1, pltpu.roll(x, shift, 1), pltpu.roll(x, 128 - shift, 1))


def chip_kernel(mine, theirs, out):
    out[0] = mine[0] + theirs[0]


def pair_kernel(mine, theirs, out):
    core = lax.rem(lax.axis_index(AXIS), 2)
    out[...] = mine[0] + turn(theirs[0], 6, core)


def far_kernel(mine, theirs, out):
    core = lax.rem(lax.axis_index(AXIS), 2)
    out[...] = mine[...] + turn(theirs[...], 12, core)


def coarse(W):
    n = 48
    I, J = iota((n, 128), 0).astype(F32), iota((n, 128), 1).astype(F32)
    lane = J[0:1]
    Wt = jnp.transpose(jnp.concatenate([W, jnp.zeros((120, 128), F32)], axis=0))[0:n]
    row = [W[k : k + 1] for k in range(6)]
    col = [Wt[:, k : k + 1] for k in range(6)]
    to = [(col[4 + s] + I) == J for s in range(2)]
    fro = [(row[4 + s] + lane) == I for s in range(2)]
    r_row = row[0] + jnp.sum(
        jnp.where(to[0], col[2], 0.0) + jnp.where(to[1], col[3], 0.0), axis=0, keepdims=True
    )
    r_col = col[0] + jnp.sum(
        jnp.where(fro[0], row[2], 0.0) + jnp.where(fro[1], row[3], 0.0), axis=1, keepdims=True
    )
    links = to[0].astype(F32) + to[1].astype(F32)
    diag = jnp.where(I == J, 0.2, 0.0)
    g_row, g_col = 0.8 * r_row * row[1], 0.8 * r_col * col[1]
    m_row = links * (819.2 * row[1]) + diag
    m_col = links * (819.2 * col[1]) + diag
    x = g_col
    x = g_row + jnp.sum(m_row * x, axis=0, keepdims=True)
    x = g_col + jnp.sum(m_col * x, axis=1, keepdims=True)
    return g_row + jnp.sum(m_row * x, axis=0, keepdims=True)


def main_kernel(
    devices, conc, pot, strips, got_e, got_o, w_mine, w_theirs, rows_s, home_s, match_s, diff_s,
    end_out, pot_out, U, G, Q, ST, DV, DH, MIDS, CR, sem, st_sem, out_sem,
):
    me = lax.axis_index(AXIS)
    core = lax.rem(me, 2)

    def copies(b):
        out = []
        for j in range(NT):
            cols = pl.ds(128 * j, 128)
            out.append(pltpu.make_async_copy(conc.at[b, :, :, cols], U.at[b, :, j, pl.ds(LO, ROWS), :], sem.at[b]))
            out.append(pltpu.make_async_copy(pot.at[b, :, cols], G.at[b, j, pl.ds(LO, ROWS), :], sem.at[b]))
        return out

    def results(b):
        out = []
        for j in range(NT):
            cols = pl.ds(128 * j, 128)
            out.append(pltpu.make_async_copy(U.at[b, :, j, pl.ds(LO, ROWS), :], end_out.at[b, :, :, cols], out_sem.at[b]))
            out.append(pltpu.make_async_copy(G.at[b, j, pl.ds(LO, ROWS), :], pot_out.at[b, :, cols], out_sem.at[b]))
        return out

    halo = [
        pltpu.make_async_copy(strips, ST.at[pl.ds(0, 6)], st_sem.at[0]),
        pltpu.make_async_copy(got_e.at[pl.ds(0, NT)], ST.at[6], st_sem.at[1]),
        pltpu.make_async_copy(got_o.at[pl.ds(0, NT)], ST.at[7], st_sem.at[2]),
    ]
    for c in halo:
        c.start()
    for b in range(B):
        for c in copies(b):
            c.start()

    l8, s8 = iota((8, 128), 1), iota((8, 128), 0)
    in_chip = (l8 >= MID) & (l8 < MID + 6)
    W = w_mine[...] + jnp.where(in_chip, 0.0, w_theirs[...])
    CR[...] = jnp.broadcast_to(coarse(W), (8, 128))
    for c in halo:
        c.wait()

    rowid = iota((ROWS, 128), 0)
    first, last = l8 == 0, l8 == 127
    zero = jnp.zeros((8, 128), F32)

    def at(i):
        return pl.ds(4 + i, 8, stride=NI)

    def up(x):
        return x[1:] + [pltpu.roll(x[0], 7, 0)]

    def down(x):
        return [pltpu.roll(x[NI - 1], 1, 0)] + x[:-1]

    def right_of(x, nxt):
        return [
            jnp.where(last, zero if nxt is None else pltpu.roll(nxt[i], 127, 1), pltpu.roll(x[i], 127, 1))
            for i in range(NI)
        ]

    def left_of(x, prv):
        return [
            jnp.where(first, zero if prv is None else pltpu.roll(prv[i], 1, 1), pltpu.roll(x[i], 1, 1))
            for i in range(NI)
        ]

    def block(b, _):
        for c in copies(b):
            c.wait()
        n = rows_s[b]
        info = [face_info(match_s, home_s, b, side, me, devices) for side in range(2)]
        live = rowid < n
        for j in range(NT):
            G[b, j, LO : LO + ROWS, :] = jnp.where(live, G[b, j, LO : LO + ROWS, :], 0.0)
            c = []
            for s in range(S):
                x = jnp.where(live, U[b, s, j, LO : LO + ROWS, :], 0.0)
                U[b, s, j, LO : LO + ROWS, :] = x
                U[b, s, j, 0:LO, :] = zero
                U[b, s, j, LO + ROWS : H, :] = zero
                c.append(x)
            Q[b, j, LO : LO + ROWS, :] = c[0] - c[1] + 2.0 * c[2] - c[3]
            for ref in (G, Q):
                ref[b, j, 0:LO, :] = zero
                ref[b, j, LO + ROWS : H, :] = zero
        for side in range(2):
            is_open, off, pb, pf, _, _ = info[side]
            src = jnp.where(off == 1, 2 * pb + pf, jnp.where(off == 2 - 2 * core, 6, 7))

            @pl.when(is_open)
            def _():
                for k in range(4):
                    row = pl.ds(LO - 1 - k if side == 0 else LO + n + k, 1)
                    G[b, :, row, :] = ST[src, :, k : k + 1, :]
                    if k < 3:
                        Q[b, :, row, :] = ST[src, :, 4 + k : 5 + k, :]
                    if k < 2:
                        for s in range(S):
                            U[b, s, :, row, :] = ST[src, :, 7 + 2 * s + k : 8 + 2 * s + k, :]

        lane_own = MID + B * core + b
        cr = CR[...]

        def pick(l):
            return jnp.sum(jnp.where(l8 == l, cr, 0.0), axis=1, keepdims=True)

        c_own = pick(lane_own)
        c_side = [pick(lane_own + i[5]) for i in info]
        lo = jnp.where(info[0][0], -4, 0)
        hi = jnp.where(info[1][0], n + 3, n - 1)
        w_in, w_edge, corr, alive, linked = [], [], [], [], []
        for i in range(NI):
            r = NI * s8 + (i - 4)
            inside = (r >= lo) & (r <= hi)
            wall = ((r == 0) & (lo == 0)) | ((r == n - 1) & (hi == n - 1))
            links = jnp.where(wall, 1.0, 2.0)
            w_in.append(jnp.where(inside, 0.8 / (2.5 + links), 0.0))
            w_edge.append(jnp.where(inside, 0.8 / (1.5 + links), 0.0))
            c = jnp.where(r < 0, c_side[0], jnp.where(r >= n, c_side[1], c_own))
            corr.append(jnp.where(inside, c, 0.0))
            alive.append((r >= 0) & (r < n))
            linked.append(jnp.logical_not(((r == -1) & (lo == 0)) | ((r == n - 1) & (hi == n - 1))))

        def weight(i, j):
            if j == 0:
                return jnp.where(first, w_edge[i], w_in[i])
            if j == NT - 1:
                return jnp.where(last, w_edge[i], w_in[i])
            return w_in[i]

        def smooth(load, store):
            prv, cur = None, [load(i, 0) for i in range(NI)]
            for j in range(NT):
                nxt = [load(i, j + 1) for i in range(NI)] if j < NT - 1 else None
                u, d, lf, rt = up(cur), down(cur), left_of(cur, prv), right_of(cur, nxt)
                for i in range(NI):
                    q = Q[b, j, at(i), :]
                    store(i, j, 0.2 * cur[i] + weight(i, j) * (q + ((u[i] + d[i]) + (lf[i] + rt[i]))))
                prv, cur = cur, nxt

        def put_v(i, j, x):
            MIDS[i, j] = x + corr[i]

        def put_phi(i, j, x):
            DV[i, j] = x

        smooth(lambda i, j: G[b, j, at(i), :], put_v)
        smooth(lambda i, j: MIDS[i, j], put_phi)
        cur = [DV[i, 0] for i in range(NI)]
        for j in range(NT):
            nxt = [DV[i, j + 1] for i in range(NI)] if j < NT - 1 else None
            u, rt = up(cur), right_of(cur, nxt)
            for i in range(NI):
                G[b, j, at(i), :] = jnp.where(alive[i], cur[i], 0.0)
                DV[i, j] = u[i] - cur[i]
                DH[i, j] = rt[i] - cur[i]
            cur = nxt

        def species(s, _):
            half_z = jnp.where(s == 0, 0.5, jnp.where(s == 2, 1.0, -0.5)).astype(F32)
            k1 = 0.1 * diff_s[s]

            def stage(load, store):
                prv, cur = None, [load(i, 0) for i in range(NI)]
                for j in range(NT):
                    nxt = [load(i, j + 1) for i in range(NI)] if j < NT - 1 else None
                    u, rt = up(cur), right_of(cur, nxt)
                    fv, fh = [], []
                    for i in range(NI):
                        f = (u[i] - cur[i]) + (u[i] + cur[i]) * (half_z * DV[i, j])
                        fv.append(jnp.where(linked[i], f, 0.0))
                        f = (rt[i] - cur[i]) + (rt[i] + cur[i]) * (half_z * DH[i, j])
                        fh.append(jnp.where(last, 0.0, f) if j == NT - 1 else f)
                    fd, fl = down(fv), left_of(fh, prv)
                    for i in range(NI):
                        store(i, j, cur[i], (fv[i] - fd[i]) + (fh[i] - fl[i]))
                    prv, cur = fh, nxt

            def put_mid(i, j, u, rate):
                MIDS[i, j] = u + k1 * rate

            def put_end(i, j, mid, rate):
                u = U[b, s, j, at(i), :]
                x = 0.5 * u + 0.5 * (mid + k1 * rate)
                U[b, s, j, at(i), :] = jnp.where(alive[i], x, 0.0)

            stage(lambda i, j: U[b, s, j, at(i), :], put_mid)
            stage(lambda i, j: MIDS[i, j], put_end)
            return 0

        lax.fori_loop(0, S, species, 0)
        for c in results(b):
            c.start()
        return 0

    lax.fori_loop(0, B, block, 0)
    for b in range(B):
        for c in results(b):
            c.wait()


ANY = pl.BlockSpec(memory_space=pl.ANY)
SMEM = pl.BlockSpec(memory_space=pltpu.SMEM)
VMEM = pl.BlockSpec(memory_space=pltpu.VMEM)
PARAMS = pltpu.CompilerParams(vmem_limit_bytes=40 * 1024 * 1024)


def shaped(*shape):
    return jax.ShapeDtypeStruct(shape, F32)


def body(concentration, potential_guess, diffusivity, block_rows, block_home, face_match):
    devices = lax.axis_size(AXIS)

    def swap(x, pairs):
        return lax.ppermute(x, AXIS, pairs)

    on_chip = [(i, i ^ 1) for i in range(devices)]
    off_chip = [(i, (i + 1 if i % 2 else i - 1) % devices) for i in range(devices)]
    beyond = [((i + 4 if i % 2 else i - 4) % devices, i) for i in range(devices)]

    strips, msg_e, msg_o = pl.pallas_call(
        functools.partial(pack_kernel, devices),
        out_shape=(shaped(2 * B, NT, 16, 128), shaped(NT + 1, 16, 128), shaped(NT + 1, 16, 128)),
        in_specs=[ANY, ANY, SMEM, SMEM, SMEM],
        out_specs=(VMEM, VMEM, VMEM),
        scratch_shapes=[
            pltpu.VMEM((B, S, NT, H, 128), F32),
            pltpu.VMEM((B, NT, H, 128), F32),
            pltpu.VMEM((B, NT, H, 128), F32),
            pltpu.SemaphoreType.DMA((B,)),
        ],
        compiler_params=PARAMS,
        name="pack",
    )(concentration, potential_guess, block_rows, block_home, face_match)

    got_e = swap(msg_e, on_chip)
    record = pl.BlockSpec((1, 8, 128), lambda i: (NT, 0, 0))
    whole = pl.BlockSpec((8, 128), lambda i: (0, 0))
    msg_o = pl.pallas_call(
        chip_kernel,
        grid=(1,),
        out_shape=shaped(NT + 1, 16, 128),
        in_specs=[record, record],
        out_specs=record,
        input_output_aliases={0: 0},
        name="chip",
    )(msg_o, got_e)
    got_o = swap(msg_o, off_chip)
    w1 = pl.pallas_call(
        pair_kernel,
        grid=(1,),
        out_shape=shaped(8, 128),
        in_specs=[record, record],
        out_specs=whole,
        name="pair",
    )(msg_o, got_o)
    w2 = pl.pallas_call(
        far_kernel,
        out_shape=shaped(8, 128),
        in_specs=[VMEM, VMEM],
        out_specs=VMEM,
        name="far",
    )(w1, swap(w1, beyond))
    w_other = swap(w2, on_chip)

    return pl.pallas_call(
        functools.partial(main_kernel, devices),
        out_shape=(shaped(B, S, ROWS, FACE), shaped(B, ROWS, FACE)),
        in_specs=[ANY] * 5 + [VMEM, VMEM] + [SMEM] * 4,
        out_specs=(ANY, ANY),
        scratch_shapes=[
            pltpu.VMEM((B, S, NT, H, 128), F32),
            pltpu.VMEM((B, NT, H, 128), F32),
            pltpu.VMEM((B, NT, H, 128), F32),
            pltpu.VMEM((8, NT, 16, 128), F32),
            pltpu.VMEM((NI, NT, 8, 128), F32),
            pltpu.VMEM((NI, NT, 8, 128), F32),
            pltpu.VMEM((NI, NT, 8, 128), F32),
            pltpu.VMEM((8, 128), F32),
            pltpu.SemaphoreType.DMA((B,)),
            pltpu.SemaphoreType.DMA((3,)),
            pltpu.SemaphoreType.DMA((B,)),
        ],
        compiler_params=PARAMS,
        name="transport",
    )(
        concentration, potential_guess, strips, got_e, got_o, w2, w_other,
        block_rows, block_home, face_match, diffusivity,
    )


def solution(mesh):
    in_specs = (
        P("blk", None, None, None),
        P("blk", None, None),
        P(),
        P("blk"),
        P(),
        P("blk", None, None),
    )
    out_specs = (P("blk", None, None, None), P("blk", None, None))
    return jax.shard_map(body, mesh=mesh, in_specs=in_specs, out_specs=out_specs, check_vma=False)
```

time: 206 us -> 64.2 us (0.31)
  the two profiles are of different devices: /device:TPU:32 before, /device:TPU:1 now
where the time goes in v1:
time: 64.2 us; the launch traced here: 63.6 us
  starting transfers between devices  30.8 us (48%)
  Pallas kernels  15.7 us (24%)
  local copies, waits for them, and re-layouts  9.54 us (15%)
  waiting for transfers between devices  6.8 us (11%)
  between operations  0.75 us (1%)
    ppermute x4, starting transfers between devices, swap(): return lax.ppermute(x, AXIS, pairs)  30.8 us
    unnamed x36, local copies, waits for them, and re-layouts  9.54 us
    pallas_call x1, Pallas kernels, body(): pl.pallas_call(functools.partial(main_kernel, devices), out_shape=(shaped...  9.2 us
    ppermute x4, waiting for transfers between devices, swap(): return lax.ppermute(x, AXIS, pairs)  6.8 us
    pallas_call x1, Pallas kernels, body(): pl.pallas_call(functools.partial(pack_kernel, devices), out_shape=(shaped...  2.45 us
    pallas_call x1, Pallas kernels, body(): pl.pallas_call(pair_kernel, grid=(1,), out_shape=shaped(8, 128), in_specs...  1.38 us
    pallas_call x1, Pallas kernels, body(): pl.pallas_call(far_kernel, out_shape=shaped(8, 128), in_specs=[VMEM, VMEM...  1.34 us
    pallas_call x1, Pallas kernels, body(): pl.pallas_call(chip_kernel, grid=(1,), out_shape=shaped(NT + 1, 16, 128),...  1.3 us
  transfers between devices with their start and end apart: 4, of which 4 were waited for; matrix products, arithmetic and copies ran while one was open for 0% of the time, Pallas kernels for 0%

profile of v1, /device:TPU:1, one launch (start us, length us, event | category | flops | bytes accessed | tf_op | source)
XLA Modules:
  0.0 63.6 jit_solution(12799651993888954680)
XLA Ops:
  0.6 0.0 copy-start
  0.6 1.5 %copy-done = f32[3,4,40,1024]{3,2,1,0:T(8,128)S(1)} copy-done((f32[3,4,40,1024]{3,2,1,0:T(8,128)S(1)}, f32[3,4,40,1024]{3,2,1,0:T(8,128)}, u32[]{:S(2)}) %copy-start) | copy-done | bytes 1966104
  2.2 0.0 copy-start.2
  2.2 1.0 %copy-done.2 = f32[3,40,1024]{2,1,0:T(8,128)S(1)} copy-done((f32[3,40,1024]{2,1,0:T(8,128)S(1)}, f32[3,40,1024]{2,1,0:T(8,128)}, u32[]{:S(2)}) %copy-start.2) | copy-done | bytes 491544
  3.2 0.0 copy-start.9
  3.2 0.7 %copy-done.9 = s32[1536]{0:T(1024)S(1)} copy-done((s32[1536]{0:T(1024)S(1)}, s32[1536]{0:T(1024)}, u32[]{:S(2)}) %copy-start.9) | copy-done | bytes 6168
  3.9 0.0 copy-start.12
  3.9 0.7 %copy-done.12 = s32[3,2,3]{2,1,0:T(2,128)S(1)} copy-done((s32[3,2,3]{2,1,0:T(2,128)S(1)}, s32[3,2,3]{2,1,0:T(2,128)}, u32[]{:S(2)}) %copy-start.12) | copy-done | bytes 96
  4.6 0.0 copy-start.14
  4.6 0.7 %copy-done.14 = s32[3]{0:T(128)S(1)} copy-done((s32[3]{0:T(128)S(1)}, s32[3]{0:T(128)}, u32[]{:S(2)}) %copy-start.14) | copy-done | bytes 36
  5.2 0.0 copy-start.1
  5.2 0.0 copy-start.3
  5.3 0.0 copy-start.10
  5.3 0.0 copy-start.13
  5.3 0.0 copy-start.15
  5.3 0.0 copy-start.16
  5.3 2.4 %pack.1 = (f32[6,8,16,128]{3,2,1,0:T(8,128)S(1)}, f32[9,16,128]{2,1,0:T(8,128)S(1)}, f32[9,16,128]{2,1,0:T(8,128)S(1)}) custom-call(f32[3,4,40,1024]{3,2,1,0:T(8,128)S(1)} %copy-done, f32[3,40,1024]{2,1,0:T(8,128)S(1)} %copy-done.2, s32[3]{0:T(128)S(1)} %copy-done.14, s32[1536]{0:T(1024)S(1)} %copy-done.9, s32[3,2,3]{2,1,0:T(2,128)S(1)} %copy-done.12), custom_call_target="tpu_custom_call" | custom-call | tf_op jit(solution)/shard_map/pack/pallas_call | solution.py:419
  7.7 0.0 copy-start.8
  7.7 0.6 copy-done.8
  8.4 8.7 %collective-permute-start = (f32[9,16,128]{2,1,0:T(8,128)S(1)}, f32[9,16,128]{2,1,0:T(8,128)S(1)}, u32[]{:S(2)}, u32[]{:S(2)}) collective-permute-start(f32[9,16,128]{2,1,0:T(8,128)S(1)} %get-tuple-element.6), channel_id=1, source_target_pairs={{0,1},{1,0},{2,3},{3,2},{4,5},{5,4},{6,7},{7,6},{8,9},{9,8},{10,11... | collective-permute-start | bytes 221192 | tf_op jit(solution)/shard_map/ppermute | solution.py:413
  17.1 0.9 %collective-permute-done.theirs.got_e = f32[9,16,128]{2,1,0:T(8,128)S(1)} collective-permute-done((f32[9,16,128]{2,1,0:T(8,128)S(1)}, f32[9,16,128]{2,1,0:T(8,128)S(1)}, u32[]{:S(2)}, u32[]{:S(2)}) %collective-permute-start) | collective-permute-done | bytes 73760 | tf_op jit(solution)/shard_map/ppermute | solution.py:413
  18.0 0.0 copy-start.4
  18.0 0.6 copy-done.4
  18.6 1.3 %chip.1.mine = f32[9,16,128]{2,1,0:T(8,128)} custom-call(f32[9,16,128]{2,1,0:T(8,128)} %copy-done.8, f32[9,16,128]{2,1,0:T(8,128)} %copy-done.4), custom_call_target="tpu_custom_call", output_to_operand_aliasing={{}: (0, {})} | custom-call | tf_op jit(solution)/shard_map/chip/pallas_call | solution.py:437
  19.9 1.9 %collective-permute-start.1 = (f32[9,16,128]{2,1,0:T(8,128)}, f32[9,16,128]{2,1,0:T(8,128)S(1)}, u32[]{:S(2)}, u32[]{:S(2)}) collective-permute-start(f32[9,16,128]{2,1,0:T(8,128)} %chip.1.mine), channel_id=1, source_target_pairs={{0,511},{1,2},{2,1},{3,4},{4,3},{5,6},{6,5},{7,8},{8,7},{9,10},{10... | collective-permute-start | bytes 221192 | tf_op jit(solution)/shard_map/ppermute | solution.py:413
  21.8 4.0 %collective-permute-done.1.theirs.got_o = f32[9,16,128]{2,1,0:T(8,128)S(1)} collective-permute-done((f32[9,16,128]{2,1,0:T(8,128)}, f32[9,16,128]{2,1,0:T(8,128)S(1)}, u32[]{:S(2)}, u32[]{:S(2)}) %collective-permute-start.1) | collective-permute-done | bytes 73760 | tf_op jit(solution)/shard_map/ppermute | solution.py:413
  25.8 0.0 copy-start.6
  25.8 0.6 copy-done.6
  26.4 1.4 %pair.1.mine = f32[8,128]{1,0:T(8,128)} custom-call(f32[9,16,128]{2,1,0:T(8,128)} %chip.1.mine, f32[9,16,128]{2,1,0:T(8,128)} %copy-done.6), custom_call_target="tpu_custom_call" | custom-call | tf_op jit(solution)/shard_map/pair/pallas_call | solution.py:447
  27.8 10.4 %collective-permute-start.2 = (f32[8,128]{1,0:T(8,128)}, f32[8,128]{1,0:T(8,128)S(1)}, u32[]{:S(2)}, u32[]{:S(2)}) collective-permute-start(f32[8,128]{1,0:T(8,128)} %pair.1.mine), channel_id=1, source_target_pairs={{508,0},{5,1},{510,2},{7,3},{0,4},{9,5},{2,6},{11,7},{4,8},{13,9},... | collective-permute-start | bytes 12296 | tf_op jit(solution)/shard_map/ppermute | solution.py:413
  38.2 0.9 %collective-permute-done.2.theirs = f32[8,128]{1,0:T(8,128)S(1)} collective-permute-done((f32[8,128]{1,0:T(8,128)}, f32[8,128]{1,0:T(8,128)S(1)}, u32[]{:S(2)}, u32[]{:S(2)}) %collective-permute-start.2) | collective-permute-done | bytes 4128 | tf_op jit(solution)/shard_map/ppermute | solution.py:413
  39.1 0.0 copy-start.17
  39.1 0.6 copy-done.17
  39.7 1.3 %far.1.w_mine = f32[8,128]{1,0:T(8,128)} custom-call(f32[8,128]{1,0:T(8,128)} %pair.1.mine, f32[8,128]{1,0:T(8,128)} %copy-done.17), custom_call_target="tpu_custom_call" | custom-call | tf_op jit(solution)/shard_map/far/pallas_call | solution.py:455
  41.0 9.9 %collective-permute-start.3 = (f32[8,128]{1,0:T(8,128)}, f32[8,128]{1,0:T(8,128)S(1)}, u32[]{:S(2)}, u32[]{:S(2)}) collective-permute-start(f32[8,128]{1,0:T(8,128)} %far.1.w_mine), channel_id=1, source_target_pairs={{0,1},{1,0},{2,3},{3,2},{4,5},{5,4},{6,7},{7,6},{8,9},{9,8},{10,11... | collective-permute-start | bytes 12296 | tf_op jit(solution)/shard_map/ppermute | solution.py:413
  50.9 1.0 %collective-permute-done.3.w_theirs = f32[8,128]{1,0:T(8,128)S(1)} collective-permute-done((f32[8,128]{1,0:T(8,128)}, f32[8,128]{1,0:T(8,128)S(1)}, u32[]{:S(2)}, u32[]{:S(2)}) %collective-permute-start.3) | collective-permute-done | bytes 4128 | tf_op jit(solution)/shard_map/ppermute | solution.py:413
  51.9 0.0 copy-done.1
  51.9 0.0 copy-done.3
  51.9 0.0 copy-done.10
  51.9 0.0 copy-done.13
  51.9 0.0 copy-done.15
  51.9 0.0 copy-done.16
  51.9 0.0 copy-start.5
  52.0 0.9 %copy-done.5 = f32[9,16,128]{2,1,0:T(8,128)S(1)} copy-done((f32[9,16,128]{2,1,0:T(8,128)S(1)}, f32[9,16,128]{2,1,0:T(8,128)}, u32[]{:S(2)}) %copy-start.5) | copy-done | bytes 73752
  52.8 0.0 copy-start.7
  52.8 0.9 %copy-done.7 = f32[9,16,128]{2,1,0:T(8,128)S(1)} copy-done((f32[9,16,128]{2,1,0:T(8,128)S(1)}, f32[9,16,128]{2,1,0:T(8,128)}, u32[]{:S(2)}) %copy-start.7) | copy-done | bytes 73752
  53.7 0.7 %copy-done.11 = f32[8,128]{1,0:T(8,128)S(1)} copy-done((f32[8,128]{1,0:T(8,128)S(1)}, f32[8,128]{1,0:T(8,128)}, u32[]{:S(2)}) %copy-start.11) | copy-done | bytes 4120
  54.4 9.2 %transport.1 = (f32[3,4,40,1024]{3,2,1,0:T(8,128)}, f32[3,40,1024]{2,1,0:T(8,128)}) custom-call(f32[3,4,40,1024]{3,2,1,0:T(8,128)S(1)} %copy-done.1, f32[3,40,1024]{2,1,0:T(8,128)S(1)} %copy-done.3, f32[6,8,16,128]{3,2,1,0:T(8,128)S(1)} %get-tuple-element.5.strips, f32[9,16,128]{2,1,0:T(8,128)S(1)} %copy-done.5, f32[9,16,128]{2,1,0:T(8,128)S(1)} %copy-done.7, ...), custom_call_target="tpu_custom_call" | custom-call | tf_op jit(solution)/shard_map/transport/pallas_call | solution.py:464
  (1 shorter events, 0.0 us)
Async XLA Ops:
  0.6 1.5 %copy-start = (f32[3,4,40,1024]{3,2,1,0:T(8,128)S(1)}, f32[3,4,40,1024]{3,2,1,0:T(8,128)}, u32[]{:S(2)}) copy-start(f32[3,4,40,1024]{3,2,1,0:T(8,128)} %conc.3) | copy-start | bytes 5898244
  2.2 1.0 %copy-start.2 = (f32[3,40,1024]{2,1,0:T(8,128)S(1)}, f32[3,40,1024]{2,1,0:T(8,128)}, u32[]{:S(2)}) copy-start(f32[3,40,1024]{2,1,0:T(8,128)} %pot.3) | copy-start | bytes 1474564
  3.2 0.7 %copy-start.9 = (s32[1536]{0:T(1024)S(1)}, s32[1536]{0:T(1024)}, u32[]{:S(2)}) copy-start(s32[1536]{0:T(1024)} %home_s.3) | copy-start | bytes 18436
  3.9 0.7 %copy-start.12 = (s32[3,2,3]{2,1,0:T(2,128)S(1)}, s32[3,2,3]{2,1,0:T(2,128)}, u32[]{:S(2)}) copy-start(s32[3,2,3]{2,1,0:T(2,128)} %match_s.3) | copy-start | bytes 220
  4.6 0.7 %copy-start.14 = (s32[3]{0:T(128)S(1)}, s32[3]{0:T(128)}, u32[]{:S(2)}) copy-start(s32[3]{0:T(128)} %rows_s.3) | copy-start | bytes 40
  5.2 46.7 %copy-start.1 = (f32[3,4,40,1024]{3,2,1,0:T(8,128)S(1)}, f32[3,4,40,1024]{3,2,1,0:T(8,128)}, u32[]{:S(2)}) copy-start(f32[3,4,40,1024]{3,2,1,0:T(8,128)} %conc.3) | copy-start | bytes 5898244
  5.2 46.7 %copy-start.3 = (f32[3,40,1024]{2,1,0:T(8,128)S(1)}, f32[3,40,1024]{2,1,0:T(8,128)}, u32[]{:S(2)}) copy-start(f32[3,40,1024]{2,1,0:T(8,128)} %pot.3) | copy-start | bytes 1474564
  5.3 46.7 %copy-start.10 = (s32[1536]{0:T(1024)S(1)}, s32[1536]{0:T(1024)}, u32[]{:S(2)}) copy-start(s32[1536]{0:T(1024)} %home_s.3) | copy-start | bytes 18436
  5.3 46.7 %copy-start.13 = (s32[3,2,3]{2,1,0:T(2,128)S(1)}, s32[3,2,3]{2,1,0:T(2,128)}, u32[]{:S(2)}) copy-start(s32[3,2,3]{2,1,0:T(2,128)} %match_s.3) | copy-start | bytes 220
  5.3 46.7 %copy-start.15 = (s32[3]{0:T(128)S(1)}, s32[3]{0:T(128)}, u32[]{:S(2)}) copy-start(s32[3]{0:T(128)} %rows_s.3) | copy-start | bytes 40
  5.3 46.7 %copy-start.16 = (f32[4]{0:T(128)S(1)}, f32[4]{0:T(128)}, u32[]{:S(2)}) copy-start(f32[4]{0:T(128)} %diff_s.1) | copy-start | bytes 52
  7.7 0.6 copy-start.8
  8.4 9.6 %collective-permute-start = (f32[9,16,128]{2,1,0:T(8,128)S(1)}, f32[9,16,128]{2,1,0:T(8,128)S(1)}, u32[]{:S(2)}, u32[]{:S(2)}) collective-permute-start(f32[9,16,128]{2,1,0:T(8,128)S(1)} %get-tuple-element.6), channel_id=1, source_target_pairs={{0,1},{1,0},{2,3},{3,2},{4,5},{5,4},{6,7},{7,6},{8,9},{9,8},{10,11... | collective-permute-start | bytes 221192 | tf_op jit(solution)/shard_map/ppermute | solution.py:413
  18.0 0.6 copy-start.4
  19.9 5.9 %collective-permute-start.1 = (f32[9,16,128]{2,1,0:T(8,128)}, f32[9,16,128]{2,1,0:T(8,128)S(1)}, u32[]{:S(2)}, u32[]{:S(2)}) collective-permute-start(f32[9,16,128]{2,1,0:T(8,128)} %chip.1.mine), channel_id=1, source_target_pairs={{0,511},{1,2},{2,1},{3,4},{4,3},{5,6},{6,5},{7,8},{8,7},{9,10},{10... | collective-permute-start | bytes 221192 | tf_op jit(solution)/shard_map/ppermute | solution.py:413
  25.8 0.6 copy-start.6
  27.8 11.3 %collective-permute-start.2 = (f32[8,128]{1,0:T(8,128)}, f32[8,128]{1,0:T(8,128)S(1)}, u32[]{:S(2)}, u32[]{:S(2)}) collective-permute-start(f32[8,128]{1,0:T(8,128)} %pair.1.mine), channel_id=1, source_target_pairs={{508,0},{5,1},{510,2},{7,3},{0,4},{9,5},{2,6},{11,7},{4,8},{13,9},... | collective-permute-start | bytes 12296 | tf_op jit(solution)/shard_map/ppermute | solution.py:413
  39.1 0.6 copy-start.17
  41.0 10.9 %collective-permute-start.3 = (f32[8,128]{1,0:T(8,128)}, f32[8,128]{1,0:T(8,128)S(1)}, u32[]{:S(2)}, u32[]{:S(2)}) collective-permute-start(f32[8,128]{1,0:T(8,128)} %far.1.w_mine), channel_id=1, source_target_pairs={{0,1},{1,0},{2,3},{3,2},{4,5},{5,4},{6,7},{7,6},{8,9},{9,8},{10,11... | collective-permute-start | bytes 12296 | tf_op jit(solution)/shard_map/ppermute | solution.py:413
  51.9 0.9 %copy-start.5 = (f32[9,16,128]{2,1,0:T(8,128)S(1)}, f32[9,16,128]{2,1,0:T(8,128)}, u32[]{:S(2)}) copy-start(f32[9,16,128]{2,1,0:T(8,128)} %copy-done.4) | copy-start | bytes 221188
  52.8 0.9 %copy-start.7 = (f32[9,16,128]{2,1,0:T(8,128)S(1)}, f32[9,16,128]{2,1,0:T(8,128)}, u32[]{:S(2)}) copy-start(f32[9,16,128]{2,1,0:T(8,128)} %copy-done.6) | copy-start | bytes 221188
  53.7 0.7 %copy-start.11 = (f32[8,128]{1,0:T(8,128)S(1)}, f32[8,128]{1,0:T(8,128)}, u32[]{:S(2)}) copy-start(f32[8,128]{1,0:T(8,128)} %far.1.w_mine) | copy-start | bytes 12292

commit v2 on v1

--- a/solution.py
+++ b/solution.py
@@ -33,7 +33,10 @@
     return lax.broadcasted_iota(jnp.int32, shape, dim)
 
 
-def pack_kernel(devices, conc, pot, rows_s, home_s, match_s, strips, msg_e, msg_o, U, G, Q, sem):
+def pack_kernel(
+    devices, conc, pot, rows, home, match, strips, msg_e, msg_o,
+    U, G, Q, rows_s, home_s, match_s, sem, tab_sem,
+):
     me = lax.axis_index(AXIS)
     core = lax.rem(me, 2)
 
@@ -45,9 +48,17 @@
             out.append(pltpu.make_async_copy(pot.at[b, :, cols], G.at[b, j, pl.ds(LO, ROWS), :], sem.at[b]))
         return out
 
+    tables = [
+        pltpu.make_async_copy(src, dst, tab_sem.at[k])
+        for k, (src, dst) in enumerate(((rows, rows_s), (home, home_s), (match, match_s)))
+    ]
+    for c in tables:
+        c.start()
     for b in range(B):
         for c in copies(b):
             c.start()
+    for c in tables:
+        c.wait()
 
     rowid = iota((ROWS, 128), 0)
     lane = iota((ROWS, 128), 1)
@@ -152,21 +163,7 @@
 
 
 def turn(x, shift, core):
-    return jnp.where(core == 1, pltpu.roll(x, shift, 1), pltpu.roll(x, 128 - shift, 1))
-
-
-def chip_kernel(mine, theirs, out):
-    out[0] = mine[0] + theirs[0]
-
-
-def pair_kernel(mine, theirs, out):
-    core = lax.rem(lax.axis_index(AXIS), 2)
-    out[...] = mine[0] + turn(theirs[0], 6, core)
-
-
-def far_kernel(mine, theirs, out):
-    core = lax.rem(lax.axis_index(AXIS), 2)
-    out[...] = mine[...] + turn(theirs[...], 12, core)
+    return jnp.where(core == 1, jnp.roll(x, shift, 1), jnp.roll(x, -shift, 1))
 
 
 def coarse(W):
@@ -196,8 +193,9 @@
 
 
 def main_kernel(
-    devices, conc, pot, strips, got_e, got_o, w_mine, w_theirs, rows_s, home_s, match_s, diff_s,
-    end_out, pot_out, U, G, Q, ST, DV, DH, MIDS, CR, sem, st_sem, out_sem,
+    devices, conc, pot, strips, got_e, got_o, w_mine, w_theirs, rows, home, match, diff,
+    end_out, pot_out, U, G, Q, ST, DV, DH, MIDS, CR, rows_s, home_s, match_s, diff_s,
+    sem, st_sem, out_sem, tab_sem,
 ):
     me = lax.axis_index(AXIS)
     core = lax.rem(me, 2)
@@ -223,7 +221,11 @@
         pltpu.make_async_copy(got_e.at[pl.ds(0, NT)], ST.at[6], st_sem.at[1]),
         pltpu.make_async_copy(got_o.at[pl.ds(0, NT)], ST.at[7], st_sem.at[2]),
     ]
-    for c in halo:
+    pairs = ((rows, rows_s), (home, home_s), (match, match_s), (diff, diff_s))
+    tables = [
+        pltpu.make_async_copy(src, dst, tab_sem.at[k]) for k, (src, dst) in enumerate(pairs)
+    ]
+    for c in tables + halo:
         c.start()
     for b in range(B):
         for c in copies(b):
@@ -233,7 +235,7 @@
     in_chip = (l8 >= MID) & (l8 < MID + 6)
     W = w_mine[...] + jnp.where(in_chip, 0.0, w_theirs[...])
     CR[...] = jnp.broadcast_to(coarse(W), (8, 128))
-    for c in halo:
+    for c in tables + halo:
         c.wait()
 
     rowid = iota((ROWS, 128), 0)
@@ -397,9 +399,14 @@
 
 
 ANY = pl.BlockSpec(memory_space=pl.ANY)
-SMEM = pl.BlockSpec(memory_space=pltpu.SMEM)
+HBM = pl.BlockSpec(memory_space=pltpu.HBM)
 VMEM = pl.BlockSpec(memory_space=pltpu.VMEM)
-PARAMS = pltpu.CompilerParams(vmem_limit_bytes=40 * 1024 * 1024)
+def limit(mib):
+    return pltpu.CompilerParams(vmem_limit_bytes=mib * 1024 * 1024)
+
+
+def tables(devices):
+    return pltpu.SMEM((B,), jnp.int32), pltpu.SMEM((devices * B,), jnp.int32), pltpu.SMEM((B, 2, 3), jnp.int32)
 
 
 def shaped(*shape):
@@ -408,64 +415,56 @@
 
 def body(concentration, potential_guess, diffusivity, block_rows, block_home, face_match):
     devices = lax.axis_size(AXIS)
+    concentration, potential_guess, block_rows, block_home, face_match, diffusivity = (
+        pltpu.with_memory_space_constraint(x, pltpu.HBM)
+        for x in (concentration, potential_guess, block_rows, block_home, face_match, diffusivity)
+    )
 
     def swap(x, pairs):
         return lax.ppermute(x, AXIS, pairs)
 
     on_chip = [(i, i ^ 1) for i in range(devices)]
     off_chip = [(i, (i + 1 if i % 2 else i - 1) % devices) for i in range(devices)]
-    beyond = [((i + 4 if i % 2 else i - 4) % devices, i) for i in range(devices)]
+    def beyond(k):
+        return [((i + k if i % 2 else i - k) % devices, i) for i in range(devices)]
+
 
     strips, msg_e, msg_o = pl.pallas_call(
         functools.partial(pack_kernel, devices),
         out_shape=(shaped(2 * B, NT, 16, 128), shaped(NT + 1, 16, 128), shaped(NT + 1, 16, 128)),
-        in_specs=[ANY, ANY, SMEM, SMEM, SMEM],
+        in_specs=[HBM] * 5,
         out_specs=(VMEM, VMEM, VMEM),
         scratch_shapes=[
             pltpu.VMEM((B, S, NT, H, 128), F32),
             pltpu.VMEM((B, NT, H, 128), F32),
             pltpu.VMEM((B, NT, H, 128), F32),
+            *tables(devices),
             pltpu.SemaphoreType.DMA((B,)),
+            pltpu.SemaphoreType.DMA((3,)),
         ],
-        compiler_params=PARAMS,
+        compiler_params=limit(40),
         name="pack",
     )(concentration, potential_guess, block_rows, block_home, face_match)
 
     got_e = swap(msg_e, on_chip)
-    record = pl.BlockSpec((1, 8, 128), lambda i: (NT, 0, 0))
-    whole = pl.BlockSpec((8, 128), lambda i: (0, 0))
-    msg_o = pl.pallas_call(
-        chip_kernel,
-        grid=(1,),
-        out_shape=shaped(NT + 1, 16, 128),
-        in_specs=[record, record],
-        out_specs=record,
-        input_output_aliases={0: 0},
-        name="chip",
-    )(msg_o, got_e)
-    got_o = swap(msg_o, off_chip)
-    w1 = pl.pallas_call(
-        pair_kernel,
-        grid=(1,),
-        out_shape=shaped(8, 128),
-        in_specs=[record, record],
-        out_specs=whole,
-        name="pair",
-    )(msg_o, got_o)
-    w2 = pl.pallas_call(
-        far_kernel,
-        out_shape=shaped(8, 128),
-        in_specs=[VMEM, VMEM],
-        out_specs=VMEM,
-        name="far",
-    )(w1, swap(w1, beyond))
+    core = lax.axis_index(AXIS) % 2
+    chip = msg_o[NT, 0:8] + got_e[NT, 0:8]
+    third = swap(chip, beyond(6))
+    second = swap(chip, beyond(4))
+    got_o = swap(msg_o.at[NT, 0:8].set(chip), off_chip)
+    w2 = (
+        chip
+        + turn(got_o[NT, 0:8], 6, core)
+        + turn(second, 12, core)
+        + turn(third, 18, core)
+    )
     w_other = swap(w2, on_chip)
 
     return pl.pallas_call(
         functools.partial(main_kernel, devices),
         out_shape=(shaped(B, S, ROWS, FACE), shaped(B, ROWS, FACE)),
-        in_specs=[ANY] * 5 + [VMEM, VMEM] + [SMEM] * 4,
-        out_specs=(ANY, ANY),
+        in_specs=[HBM] * 2 + [ANY] * 3 + [VMEM, VMEM] + [HBM] * 4,
+        out_specs=(HBM, HBM),
         scratch_shapes=[
             pltpu.VMEM((B, S, NT, H, 128), F32),
             pltpu.VMEM((B, NT, H, 128), F32),
@@ -475,11 +474,14 @@
             pltpu.VMEM((NI, NT, 8, 128), F32),
             pltpu.VMEM((NI, NT, 8, 128), F32),
             pltpu.VMEM((8, 128), F32),
+            *tables(devices),
+            pltpu.SMEM((4,), F32),
             pltpu.SemaphoreType.DMA((B,)),
             pltpu.SemaphoreType.DMA((3,)),
             pltpu.SemaphoreType.DMA((B,)),
+            pltpu.SemaphoreType.DMA((4,)),
         ],
-        compiler_params=PARAMS,
+        compiler_params=limit(40),
         name="transport",
     )(
         concentration, potential_guess, strips, got_e, got_o, w2, w_other,

time: 64.2 us -> 45.7 us (0.71)
  local copies, waits for them, and re-layouts: 9.54 us -> 0.44 us
  Pallas kernels: 15.7 us -> 11.7 us
  starting transfers between devices: 30.8 us -> 27 us
  waiting for transfers between devices: 6.8 us -> 5.43 us
    unnamed x36 -> x0, local copies, waits for them, and re-layouts: 9.54 us -> none
    pallas_call x3 -> x0, Pallas kernels: 4.02 us -> none  [the longest x1 1.38 us: body(): pl.pallas_call(pair_kernel, grid=(1,), out_shape=shaped(8, 128), in_specs...]
    ppermute x4 -> x5, starting transfers between devices: 30.8 us -> 27 us  [swap(): return lax.ppermute(x, AXIS, pairs)]
    ppermute x4 -> x5, waiting for transfers between devices: 6.8 us -> 5.43 us  [swap(): return lax.ppermute(x, AXIS, pairs)]
  transfers between devices with their start and end apart: 4 -> 5, of which waited for: 4 -> 4; matrix products, arithmetic and copies ran while one was open for 0% -> 1% of each run, Pallas kernels for 0% -> 0%
where the time goes in v2:
time: 45.7 us; the launch traced here: 45.3 us
  starting transfers between devices  27 us (59%)
  Pallas kernels  11.7 us (26%)
  waiting for transfers between devices  5.43 us (12%)
  between operations  0.7 us (2%)
    ppermute x5, starting transfers between devices, swap(): return lax.ppermute(x, AXIS, pairs)  27 us
    pallas_call x1, Pallas kernels, body(): pl.pallas_call(functools.partial(main_kernel, devices), out_shape=(shaped...  9 us
    ppermute x5, waiting for transfers between devices, swap(): return lax.ppermute(x, AXIS, pairs)  5.43 us
    pallas_call x1, Pallas kernels, body(): pl.pallas_call(functools.partial(pack_kernel, devices), out_shape=(shaped...  2.69 us
  transfers between devices with their start and end apart: 5, of which 4 were waited for; matrix products, arithmetic and copies ran while one was open for 1% of the time, Pallas kernels for 0%

profile of v2, /device:TPU:1, one launch (start us, length us, event | category | flops | bytes accessed | tf_op | source)
XLA Modules:
  0.0 45.3 jit_solution(3639060624066781195)
XLA Ops:
  0.6 2.7 %pack.1 = (f32[6,8,16,128]{3,2,1,0:T(8,128)S(1)}, f32[9,16,128]{2,1,0:T(8,128)S(1)}, f32[9,16,128]{2,1,0:T(8,128)S(1)}) custom-call(f32[3,4,40,1024]{3,2,1,0:T(8,128)} %conc.3, f32[3,40,1024]{2,1,0:T(8,128)} %pot.3, s32[3]{0:T(128)} %rows.3, s32[1536]{0:T(1024)} %home.3, s32[3,2,3]{2,1,0:T(2,128)} %match.3), custom_call_target="tpu_custom_call" | custom-call | tf_op jit(solution)/shard_map/pack/pallas_call | solution.py:432
  3.3 8.6 %collective-permute-start = (f32[9,16,128]{2,1,0:T(8,128)S(1)}, f32[9,16,128]{2,1,0:T(8,128)S(1)}, u32[]{:S(2)}, u32[]{:S(2)}) collective-permute-start(f32[9,16,128]{2,1,0:T(8,128)S(1)} %get-tuple-element.18), channel_id=1, source_target_pairs={{0,1},{1,0},{2,3},{3,2},{4,5},{5,4},{6,7},{7,6},{8,9},{9,8},{10,11... | collective-permute-start | bytes 221192 | tf_op jit(solution)/shard_map/ppermute | solution.py:424
  11.9 0.9 %collective-permute-done.got_e = f32[9,16,128]{2,1,0:T(8,128)S(1)} collective-permute-done((f32[9,16,128]{2,1,0:T(8,128)S(1)}, f32[9,16,128]{2,1,0:T(8,128)S(1)}, u32[]{:S(2)}, u32[]{:S(2)}) %collective-permute-start) | collective-permute-done | bytes 73760 | tf_op jit(solution)/shard_map/ppermute | solution.py:424
  12.8 10.3 %collective-permute-start.3 = (f32[8,128]{1,0:T(8,128)S(1)}, f32[8,128]{1,0:T(8,128)S(1)}, u32[]{:S(2)}, u32[]{:S(2)}) collective-permute-start(f32[8,128]{1,0:T(8,128)S(1)} %get-tuple-element.20), channel_id=1, source_target_pairs={{506,0},{7,1},{508,2},{9,3},{510,4},{11,5},{0,6},{13,7},{2,8},{15,... | collective-permute-start | bytes 12296 | tf_op jit(solution)/shard_map/ppermute | solution.py:424
  23.1 2.0 %collective-permute-start.2 = (f32[8,128]{1,0:T(8,128)S(1)}, f32[8,128]{1,0:T(8,128)S(1)}, u32[]{:S(2)}, u32[]{:S(2)}) collective-permute-start(f32[8,128]{1,0:T(8,128)S(1)} %get-tuple-element.20), channel_id=1, source_target_pairs={{508,0},{5,1},{510,2},{7,3},{0,4},{9,5},{2,6},{11,7},{4,8},{13,9},... | collective-permute-start | bytes 12296 | tf_op jit(solution)/shard_map/ppermute | solution.py:424
  25.2 1.9 %collective-permute-start.1 = (f32[9,16,128]{2,1,0:T(8,128)S(1)}, f32[9,16,128]{2,1,0:T(8,128)S(1)}, u32[]{:S(2)}, u32[]{:S(2)}) collective-permute-start(f32[9,16,128]{2,1,0:T(8,128)S(1)} %get-tuple-element.21), channel_id=1, source_target_pairs={{0,511},{1,2},{2,1},{3,4},{4,3},{5,6},{6,5},{7,8},{8,7},{9,10},{10... | collective-permute-start | bytes 221192 | tf_op jit(solution)/shard_map/ppermute | solution.py:424
  27.1 0.0 collective-permute-done.3
  27.1 0.1 fusion.6
  27.2 0.1 fusion.5
  27.2 1.1 %collective-permute-done.2 = f32[8,128]{1,0:T(8,128)S(1)} collective-permute-done((f32[8,128]{1,0:T(8,128)S(1)}, f32[8,128]{1,0:T(8,128)S(1)}, u32[]{:S(2)}, u32[]{:S(2)}) %collective-permute-start.2) | collective-permute-done | bytes 4128 | tf_op jit(solution)/shard_map/ppermute | solution.py:424
  28.4 0.1 fusion.8
  28.5 0.1 fusion.7
  28.5 2.6 %collective-permute-done.1.got_o = f32[9,16,128]{2,1,0:T(8,128)S(1)} collective-permute-done((f32[9,16,128]{2,1,0:T(8,128)S(1)}, f32[9,16,128]{2,1,0:T(8,128)S(1)}, u32[]{:S(2)}, u32[]{:S(2)}) %collective-permute-start.1) | collective-permute-done | bytes 73760 | tf_op jit(solution)/shard_map/ppermute | solution.py:424
  31.1 0.1 fusion.10
  31.2 0.1 fusion.9
  31.3 0.1 fusion.2.w_mine
  31.4 4.2 %collective-permute-start.4 = (f32[8,128]{1,0:T(8,128)S(1)}, f32[8,128]{1,0:T(8,128)S(1)}, u32[]{:S(2)}, u32[]{:S(2)}) collective-permute-start(f32[8,128]{1,0:T(8,128)S(1)} %fusion.2.w_mine), channel_id=1, source_target_pairs={{0,1},{1,0},{2,3},{3,2},{4,5},{5,4},{6,7},{7,6},{8,9},{9,8},{10,11... | collective-permute-start | bytes 12296 | tf_op jit(solution)/shard_map/ppermute | solution.py:424
  35.5 0.8 %collective-permute-done.4.w_theirs = f32[8,128]{1,0:T(8,128)S(1)} collective-permute-done((f32[8,128]{1,0:T(8,128)S(1)}, f32[8,128]{1,0:T(8,128)S(1)}, u32[]{:S(2)}, u32[]{:S(2)}) %collective-permute-start.4) | collective-permute-done | bytes 4128 | tf_op jit(solution)/shard_map/ppermute | solution.py:424
  36.3 9.0 %transport.1 = (f32[3,4,40,1024]{3,2,1,0:T(8,128)}, f32[3,40,1024]{2,1,0:T(8,128)}) custom-call(f32[3,4,40,1024]{3,2,1,0:T(8,128)} %conc.3, f32[3,40,1024]{2,1,0:T(8,128)} %pot.3, f32[6,8,16,128]{3,2,1,0:T(8,128)S(1)} %get-tuple-element.17.strips, f32[9,16,128]{2,1,0:T(8,128)S(1)} %collective-permute-done.got_e, ...), custom_call_target="tpu_custom_call" | custom-call | tf_op jit(solution)/shard_map/transport/pallas_call | solution.py:463
  (2 shorter events, 0.0 us)
Async XLA Ops:
  3.3 9.5 %collective-permute-start = (f32[9,16,128]{2,1,0:T(8,128)S(1)}, f32[9,16,128]{2,1,0:T(8,128)S(1)}, u32[]{:S(2)}, u32[]{:S(2)}) collective-permute-start(f32[9,16,128]{2,1,0:T(8,128)S(1)} %get-tuple-element.18), channel_id=1, source_target_pairs={{0,1},{1,0},{2,3},{3,2},{4,5},{5,4},{6,7},{7,6},{8,9},{9,8},{10,11... | collective-permute-start | bytes 221192 | tf_op jit(solution)/shard_map/ppermute | solution.py:424
  12.8 14.3 %collective-permute-start.3 = (f32[8,128]{1,0:T(8,128)S(1)}, f32[8,128]{1,0:T(8,128)S(1)}, u32[]{:S(2)}, u32[]{:S(2)}) collective-permute-start(f32[8,128]{1,0:T(8,128)S(1)} %get-tuple-element.20), channel_id=1, source_target_pairs={{506,0},{7,1},{508,2},{9,3},{510,4},{11,5},{0,6},{13,7},{2,8},{15,... | collective-permute-start | bytes 12296 | tf_op jit(solution)/shard_map/ppermute | solution.py:424
  23.1 5.3 %collective-permute-start.2 = (f32[8,128]{1,0:T(8,128)S(1)}, f32[8,128]{1,0:T(8,128)S(1)}, u32[]{:S(2)}, u32[]{:S(2)}) collective-permute-start(f32[8,128]{1,0:T(8,128)S(1)} %get-tuple-element.20), channel_id=1, source_target_pairs={{508,0},{5,1},{510,2},{7,3},{0,4},{9,5},{2,6},{11,7},{4,8},{13,9},... | collective-permute-start | bytes 12296 | tf_op jit(solution)/shard_map/ppermute | solution.py:424
  25.2 6.0 %collective-permute-start.1 = (f32[9,16,128]{2,1,0:T(8,128)S(1)}, f32[9,16,128]{2,1,0:T(8,128)S(1)}, u32[]{:S(2)}, u32[]{:S(2)}) collective-permute-start(f32[9,16,128]{2,1,0:T(8,128)S(1)} %get-tuple-element.21), channel_id=1, source_target_pairs={{0,511},{1,2},{2,1},{3,4},{4,3},{5,6},{6,5},{7,8},{8,7},{9,10},{10... | collective-permute-start | bytes 221192 | tf_op jit(solution)/shard_map/ppermute | solution.py:424
  31.4 5.0 %collective-permute-start.4 = (f32[8,128]{1,0:T(8,128)S(1)}, f32[8,128]{1,0:T(8,128)S(1)}, u32[]{:S(2)}, u32[]{:S(2)}) collective-permute-start(f32[8,128]{1,0:T(8,128)S(1)} %fusion.2.w_mine), channel_id=1, source_target_pairs={{0,1},{1,0},{2,3},{3,2},{4,5},{5,4},{6,7},{7,6},{8,9},{9,8},{10,11... | collective-permute-start | bytes 12296 | tf_op jit(solution)/shard_map/ppermute | solution.py:424

commit v3 on v2

--- a/solution.py
+++ b/solution.py
@@ -14,6 +14,7 @@
 H = 56
 NI = 6
 VALENCES = (1.0, -1.0, 2.0, -1.0)
+FAR = 152
 W_IN, W_EDGE = 0.8 / 4.5, 0.8 / 3.5
 WALL = -1000.0
 MID = 18
@@ -34,18 +35,18 @@
 
 
 def pack_kernel(
-    devices, conc, pot, rows, home, match, strips, msg_e, msg_o,
-    U, G, Q, rows_s, home_s, match_s, sem, tab_sem,
+    devices, conc, pot, rows, home, match, msg_e, msg_o, X, rows_s, home_s, match_s, sem, tab_sem,
 ):
     me = lax.axis_index(AXIS)
     core = lax.rem(me, 2)
+    U, G, Q = planes_of(X)
 
     def copies(b):
         out = []
         for j in range(NT):
             cols = pl.ds(128 * j, 128)
-            out.append(pltpu.make_async_copy(conc.at[b, :, :, cols], U.at[b, :, j, pl.ds(LO, ROWS), :], sem.at[b]))
-            out.append(pltpu.make_async_copy(pot.at[b, :, cols], G.at[b, j, pl.ds(LO, ROWS), :], sem.at[b]))
+            out.append(pltpu.make_async_copy(conc.at[b, :, :, cols], X.at[b, pl.ds(0, S), j, pl.ds(LO, ROWS), :], sem.at[b]))
+            out.append(pltpu.make_async_copy(pot.at[b, :, cols], X.at[b, 4, j, pl.ds(LO, ROWS), :], sem.at[b]))
         return out
 
     tables = [
@@ -129,41 +130,59 @@
             even = is_open & (off == 2 - 2 * core)
             odd = is_open & (off == 2 * core)
             fe, fo = jnp.where(even, f, fe), jnp.where(odd, f, fo)
+            strip = X.at[b, 6 + side]
             for k in range(4):
                 row = LO + k if side == 0 else LO + n - 1 - k
                 at = pl.ds(row, 1)
-                strips[f, :, k : k + 1, :] = G[b, :, at, :]
+                strip[:, k : k + 1, :] = G[b, :, at, :]
                 if k < 3:
-                    strips[f, :, 4 + k : 5 + k, :] = Q[b, :, at, :]
+                    strip[:, 4 + k : 5 + k, :] = Q[b, :, at, :]
                 if k < 2:
                     for s in range(S):
-                        strips[f, :, 7 + 2 * s + k : 8 + 2 * s + k, :] = U[b, s, :, at, :]
+                        strip[:, 7 + 2 * s + k : 8 + 2 * s + k, :] = U[b, s, :, at, :]
+            strip[:, 15:16, :] = jnp.zeros((NT, 1, 128), F32)
 
             @pl.when(rev == 1)
             def _():
                 for j in range(NT // 2):
                     for h in range(0, 16, 8):
-                        x = strips[f, j, h : h + 8, :]
-                        y = strips[f, NT - 1 - j, h : h + 8, :]
-                        strips[f, j, h : h + 8, :] = jnp.take_along_axis(y, mirror, axis=1)
-                        strips[f, NT - 1 - j, h : h + 8, :] = jnp.take_along_axis(x, mirror, axis=1)
+                        x = strip[j, h : h + 8, :]
+                        y = strip[NT - 1 - j, h : h + 8, :]
+                        strip[j, h : h + 8, :] = jnp.take_along_axis(y, mirror, axis=1)
+                        strip[NT - 1 - j, h : h + 8, :] = jnp.take_along_axis(x, mirror, axis=1)
 
         return W, fe, fo
 
-    for f in range(2 * B):
-        strips[f, :, 15:16, :] = jnp.zeros((NT, 1, 128), F32)
     W, fe, fo = lax.fori_loop(
         0, B, block, (jnp.zeros((8, 128), F32), jnp.int32(0), jnp.int32(0))
     )
     for msg, f in ((msg_e, fe), (msg_o, fo)):
         for j in range(NT):
-            msg[j] = strips[f, j]
+            msg[j] = X[f // 2, 6 + f % 2, j, 0:16, :]
         msg[NT, 0:8, :] = W
         msg[NT, 8:16, :] = jnp.zeros((8, 128), F32)
 
 
-def turn(x, shift, core):
-    return jnp.where(core == 1, jnp.roll(x, shift, 1), jnp.roll(x, -shift, 1))
+def planes_of(X):
+    return X, X.at[:, 4], X.at[:, 5]
+
+
+def chip_kernel(msg_o, got_e, chip):
+    chip[0:8, :] = msg_o[NT, 0:8, :] + got_e[NT, 0:8, :]
+    chip[8:, :] = jnp.zeros((FAR - 8, 128), F32)
+
+
+def stamp_kernel(_, chip, msg_o):
+    msg_o[NT, 0:8, :] = chip[0:8, :]
+
+
+def join_kernel(chip, second, third, got_o, out):
+    core = lax.rem(lax.axis_index(AXIS), 2)
+    total = chip[0:8, :]
+    for k, x in enumerate((got_o[NT, 0:8, :], second[0:8, :], third[0:8, :])):
+        shift = 6 * (k + 1)
+        total += jnp.where(core == 1, pltpu.roll(x, shift, 1), pltpu.roll(x, 128 - shift, 1))
+    out[...] = total
 
 
 def coarse(W):
@@ -192,53 +211,92 @@
     return g_row + jnp.sum(m_row * x, axis=0, keepdims=True)
 
 
+def insert(U, G, Q, b, side, n, strip):
+    for k in range(4):
+        row = pl.ds(LO - 1 - k if side == 0 else LO + n + k, 1)
+        G[b, :, row, :] = strip[0:NT, k : k + 1, :]
+        if k < 3:
+            Q[b, :, row, :] = strip[0:NT, 4 + k : 5 + k, :]
+        if k < 2:
+            for s in range(S):
+                U[b, s, :, row, :] = strip[0:NT, 7 + 2 * s + k : 8 + 2 * s + k, :]
+
+
+def prep_kernel(devices, _, got_e, rows, home, match, X, rows_s, home_s, match_s, tab_sem):
+    me = lax.axis_index(AXIS)
+    core = lax.rem(me, 2)
+    U, G, Q = planes_of(X)
+    pairs = ((rows, rows_s), (home, home_s), (match, match_s))
+    loads = [pltpu.make_async_copy(src, dst, tab_sem.at[k]) for k, (src, dst) in enumerate(pairs)]
+    for c in loads:
+        c.start()
+    for c in loads:
+        c.wait()
+    rowid = iota((ROWS, 128), 0)
+    zero = jnp.zeros((8, 128), F32)
+
+    def block(b, _):
+        n = rows_s[b]
+        live = rowid < n
+        for j in range(NT):
+            for s in range(S):
+                U[b, s, j, LO : LO + ROWS, :] = jnp.where(live, U[b, s, j, LO : LO + ROWS, :], 0.0)
+                U[b, s, j, 0:LO, :] = zero
+                U[b, s, j, LO + ROWS : H, :] = zero
+            Q[b, j, 0:LO, :] = zero
+            Q[b, j, LO + ROWS : H, :] = zero
+        for side in range(2):
+            is_open, off, pb, pf, _, _ = face_info(match_s, home_s, b, side, me, devices)
+
+            @pl.when(is_open & (off == 1))
+            def _():
+                insert(U, G, Q, b, side, n, X.at[pb, 6 + pf])
+
+            @pl.when(is_open & (off == 2 - 2 * core))
+            def _():
+                insert(U, G, Q, b, side, n, got_e)
+
+        return 0
+
+    lax.fori_loop(0, B, block, 0)
+
+
 def main_kernel(
-    devices, conc, pot, strips, got_e, got_o, w_mine, w_theirs, rows, home, match, diff,
-    end_out, pot_out, U, G, Q, ST, DV, DH, MIDS, CR, rows_s, home_s, match_s, diff_s,
-    sem, st_sem, out_sem, tab_sem,
+    devices, _, w_mine, w_theirs, got_o, rows, home, match, diff,
+    end_out, pot_out, X, LV, LH, MIDS, CR, rows_s, home_s, match_s, diff_s, out_sem, tab_sem,
 ):
     me = lax.axis_index(AXIS)
     core = lax.rem(me, 2)
-
-    def copies(b):
-        out = []
-        for j in range(NT):
-            cols = pl.ds(128 * j, 128)
-            out.append(pltpu.make_async_copy(conc.at[b, :, :, cols], U.at[b, :, j, pl.ds(LO, ROWS), :], sem.at[b]))
-            out.append(pltpu.make_async_copy(pot.at[b, :, cols], G.at[b, j, pl.ds(LO, ROWS), :], sem.at[b]))
-        return out
-
-    def results(b):
-        out = []
-        for j in range(NT):
-            cols = pl.ds(128 * j, 128)
-            out.append(pltpu.make_async_copy(U.at[b, :, j, pl.ds(LO, ROWS), :], end_out.at[b, :, :, cols], out_sem.at[b]))
-            out.append(pltpu.make_async_copy(G.at[b, j, pl.ds(LO, ROWS), :], pot_out.at[b, :, cols], out_sem.at[b]))
-        return out
-
-    halo = [
-        pltpu.make_async_copy(strips, ST.at[pl.ds(0, 6)], st_sem.at[0]),
-        pltpu.make_async_copy(got_e.at[pl.ds(0, NT)], ST.at[6], st_sem.at[1]),
-        pltpu.make_async_copy(got_o.at[pl.ds(0, NT)], ST.at[7], st_sem.at[2]),
-    ]
+    U, G, Q = planes_of(X)
+
+    def end_copies(b, s):
+        return [
+            pltpu.make_async_copy(
+                X.at[b, s, j, pl.ds(LO, ROWS), :], end_out.at[b, s, :, pl.ds(128 * j, 128)], out_sem.at[b]
+            )
+            for j in range(NT)
+        ]
+
+    def pot_copies(b):
+        return [
+            pltpu.make_async_copy(
+                X.at[b, 4, j, pl.ds(LO, ROWS), :], pot_out.at[b, :, pl.ds(128 * j, 128)], out_sem.at[b]
+            )
+            for j in range(NT)
+        ]
+
     pairs = ((rows, rows_s), (home, home_s), (match, match_s), (diff, diff_s))
-    tables = [
-        pltpu.make_async_copy(src, dst, tab_sem.at[k]) for k, (src, dst) in enumerate(pairs)
-    ]
-    for c in tables + halo:
+    loads = [pltpu.make_async_copy(src, dst, tab_sem.at[k]) for k, (src, dst) in enumerate(pairs)]
+    for c in loads:
         c.start()
-    for b in range(B):
-        for c in copies(b):
-            c.start()
 
     l8, s8 = iota((8, 128), 1), iota((8, 128), 0)
     in_chip = (l8 >= MID) & (l8 < MID + 6)
     W = w_mine[...] + jnp.where(in_chip, 0.0, w_theirs[...])
     CR[...] = jnp.broadcast_to(coarse(W), (8, 128))
-    for c in tables + halo:
+    for c in loads:
         c.wait()
 
-    rowid = iota((ROWS, 128), 0)
     first, last = l8 == 0, l8 == 127
     zero = jnp.zeros((8, 128), F32)
 
@@ -264,38 +322,13 @@
         ]
 
     def block(b, _):
-        for c in copies(b):
-            c.wait()
         n = rows_s[b]
         info = [face_info(match_s, home_s, b, side, me, devices) for side in range(2)]
-        live = rowid < n
-        for j in range(NT):
-            G[b, j, LO : LO + ROWS, :] = jnp.where(live, G[b, j, LO : LO + ROWS, :], 0.0)
-            c = []
-            for s in range(S):
-                x = jnp.where(live, U[b, s, j, LO : LO + ROWS, :], 0.0)
-                U[b, s, j, LO : LO + ROWS, :] = x
-                U[b, s, j, 0:LO, :] = zero
-                U[b, s, j, LO + ROWS : H, :] = zero
-                c.append(x)
-            Q[b, j, LO : LO + ROWS, :] = c[0] - c[1] + 2.0 * c[2] - c[3]
-            for ref in (G, Q):
-                ref[b, j, 0:LO, :] = zero
-                ref[b, j, LO + ROWS : H, :] = zero
         for side in range(2):
-            is_open, off, pb, pf, _, _ = info[side]
-            src = jnp.where(off == 1, 2 * pb + pf, jnp.where(off == 2 - 2 * core, 6, 7))
-
-            @pl.when(is_open)
+
+            @pl.when(info[side][0] & (info[side][1] == 2 * core))
             def _():
-                for k in range(4):
-                    row = pl.ds(LO - 1 - k if side == 0 else LO + n + k, 1)
-                    G[b, :, row, :] = ST[src, :, k : k + 1, :]
-                    if k < 3:
-                        Q[b, :, row, :] = ST[src, :, 4 + k : 5 + k, :]
-                    if k < 2:
-                        for s in range(S):
-                            U[b, s, :, row, :] = ST[src, :, 7 + 2 * s + k : 8 + 2 * s + k, :]
+                insert(U, G, Q, b, side, n, got_o)
 
         lane_own = MID + B * core + b
         cr = CR[...]
@@ -318,7 +351,7 @@
             c = jnp.where(r < 0, c_side[0], jnp.where(r >= n, c_side[1], c_own))
             corr.append(jnp.where(inside, c, 0.0))
             alive.append((r >= 0) & (r < n))
-            linked.append(jnp.logical_not(((r == -1) & (lo == 0)) | ((r == n - 1) & (hi == n - 1))))
+            linked.append(jnp.where(((r == -1) & (lo == 0)) | ((r == n - 1) & (hi == n - 1)), 0.0, 1.0))
 
         def weight(i, j):
             if j == 0:
@@ -341,35 +374,44 @@
             MIDS[i, j] = x + corr[i]
 
         def put_phi(i, j, x):
-            DV[i, j] = x
+            G[b, j, at(i), :] = jnp.where(alive[i], x, 0.0)
+            LV[0, i, j] = x
 
         smooth(lambda i, j: G[b, j, at(i), :], put_v)
         smooth(lambda i, j: MIDS[i, j], put_phi)
-        cur = [DV[i, 0] for i in range(NI)]
+        for c in pot_copies(b):
+            c.start()
+
+        def factors(ref, i, j, mask, step):
+            half = step * (0.5 * mask)
+            a, d = mask + half, mask - half
+            ref[0, i, j], ref[1, i, j] = a, d
+            ref[2, i, j], ref[3, i, j] = a + half, d - half
+
+        one = jnp.ones((8, 128), F32)
+        wall_right = jnp.where(last, 0.0, one)
+        cur = [LV[0, i, 0] for i in range(NI)]
         for j in range(NT):
-            nxt = [DV[i, j + 1] for i in range(NI)] if j < NT - 1 else None
+            nxt = [LV[0, i, j + 1] for i in range(NI)] if j < NT - 1 else None
             u, rt = up(cur), right_of(cur, nxt)
             for i in range(NI):
-                G[b, j, at(i), :] = jnp.where(alive[i], cur[i], 0.0)
-                DV[i, j] = u[i] - cur[i]
-                DH[i, j] = rt[i] - cur[i]
+                factors(LV, i, j, linked[i], u[i] - cur[i])
+                factors(LH, i, j, wall_right if j == NT - 1 else one, rt[i] - cur[i])
             cur = nxt
 
         def species(s, _):
-            half_z = jnp.where(s == 0, 0.5, jnp.where(s == 2, 1.0, -0.5)).astype(F32)
+            ia = jnp.where(s == 0, 0, jnp.where(s == 2, 2, 1))
+            ib = jnp.where(s == 0, 1, jnp.where(s == 2, 3, 0))
             k1 = 0.1 * diff_s[s]
+            k2 = 0.05 * diff_s[s]
 
             def stage(load, store):
                 prv, cur = None, [load(i, 0) for i in range(NI)]
                 for j in range(NT):
                     nxt = [load(i, j + 1) for i in range(NI)] if j < NT - 1 else None
                     u, rt = up(cur), right_of(cur, nxt)
-                    fv, fh = [], []
-                    for i in range(NI):
-                        f = (u[i] - cur[i]) + (u[i] + cur[i]) * (half_z * DV[i, j])
-                        fv.append(jnp.where(linked[i], f, 0.0))
-                        f = (rt[i] - cur[i]) + (rt[i] + cur[i]) * (half_z * DH[i, j])
-                        fh.append(jnp.where(last, 0.0, f) if j == NT - 1 else f)
+                    fv = [u[i] * LV[ia, i, j] - cur[i] * LV[ib, i, j] for i in range(NI)]
+                    fh = [rt[i] * LH[ia, i, j] - cur[i] * LH[ib, i, j] for i in range(NI)]
                     fd, fl = down(fv), left_of(fh, prv)
                     for i in range(NI):
                         store(i, j, cur[i], (fv[i] - fd[i]) + (fh[i] - fl[i]))
@@ -379,26 +421,27 @@
                 MIDS[i, j] = u + k1 * rate
 
             def put_end(i, j, mid, rate):
-                u = U[b, s, j, at(i), :]
-                x = 0.5 * u + 0.5 * (mid + k1 * rate)
+                x = 0.5 * (U[b, s, j, at(i), :] + mid) + k2 * rate
                 U[b, s, j, at(i), :] = jnp.where(alive[i], x, 0.0)
 
             stage(lambda i, j: U[b, s, j, at(i), :], put_mid)
             stage(lambda i, j: MIDS[i, j], put_end)
+            for c in end_copies(b, s):
+                c.start()
             return 0
 
         lax.fori_loop(0, S, species, 0)
-        for c in results(b):
-            c.start()
         return 0
 
     lax.fori_loop(0, B, block, 0)
     for b in range(B):
-        for c in results(b):
+        for c in pot_copies(b):
             c.wait()
-
-
-ANY = pl.BlockSpec(memory_space=pl.ANY)
+        for s in range(S):
+            for c in end_copies(b, s):
+                c.wait()
+
+
 HBM = pl.BlockSpec(memory_space=pltpu.HBM)
 VMEM = pl.BlockSpec(memory_space=pltpu.VMEM)
 def limit(mib):
@@ -429,15 +472,14 @@
         return [((i + k if i % 2 else i - k) % devices, i) for i in range(devices)]
 
 
-    strips, msg_e, msg_o = pl.pallas_call(
+    state = pltpu.VMEM((B, S + 4, NT, H, 128), F32)
+    message = pltpu.VMEM((NT + 1, 16, 128), F32)
+    msg_e, msg_o, x = pl.pallas_call(
         functools.partial(pack_kernel, devices),
-        out_shape=(shaped(2 * B, NT, 16, 128), shaped(NT + 1, 16, 128), shaped(NT + 1, 16, 128)),
+        out_shape=(message, message, state),
         in_specs=[HBM] * 5,
-        out_specs=(VMEM, VMEM, VMEM),
+        out_specs=(VMEM,) * 3,
         scratch_shapes=[
-            pltpu.VMEM((B, S, NT, H, 128), F32),
-            pltpu.VMEM((B, NT, H, 128), F32),
-            pltpu.VMEM((B, NT, H, 128), F32),
             *tables(devices),
             pltpu.SemaphoreType.DMA((B,)),
             pltpu.SemaphoreType.DMA((3,)),
@@ -447,46 +489,69 @@
     )(concentration, potential_guess, block_rows, block_home, face_match)
 
     got_e = swap(msg_e, on_chip)
-    core = lax.axis_index(AXIS) % 2
-    chip = msg_o[NT, 0:8] + got_e[NT, 0:8]
+    record = pltpu.VMEM((FAR, 128), F32)
+    chip = pl.pallas_call(
+        chip_kernel,
+        out_shape=record,
+        in_specs=[VMEM, VMEM],
+        out_specs=VMEM,
+        compiler_params=limit(1),
+        name="chip",
+    )(msg_o, got_e)
+    msg_o = pl.pallas_call(
+        stamp_kernel,
+        out_shape=message,
+        in_specs=[VMEM, VMEM],
+        out_specs=VMEM,
+        input_output_aliases={0: 0},
+        compiler_params=limit(1),
+        name="stamp",
+    )(msg_o, chip)
     third = swap(chip, beyond(6))
     second = swap(chip, beyond(4))
-    got_o = swap(msg_o.at[NT, 0:8].set(chip), off_chip)
-    w2 = (
-        chip
-        + turn(got_o[NT, 0:8], 6, core)
-        + turn(second, 12, core)
-        + turn(third, 18, core)
-    )
+    x = pl.pallas_call(
+        functools.partial(prep_kernel, devices),
+        out_shape=state,
+        in_specs=[VMEM] * 2 + [HBM] * 3,
+        out_specs=VMEM,
+        scratch_shapes=[*tables(devices), pltpu.SemaphoreType.DMA((3,))],
+        input_output_aliases={0: 0},
+        compiler_params=limit(40),
+        name="prep",
+    )(x, got_e, block_rows, block_home, face_match)
+    got_o = swap(msg_o, off_chip)
+    x, chip = lax.optimization_barrier((x, chip))
+    w2 = pl.pallas_call(
+        join_kernel,
+        out_shape=pltpu.VMEM((8, 128), F32),
+        in_specs=[VMEM] * 4,
+        out_specs=VMEM,
+        compiler_params=limit(1),
+        name="join",
+    )(chip, second, third, got_o)
     w_other = swap(w2, on_chip)
 
-    return pl.pallas_call(
+    link = pltpu.VMEM((4, NI, NT, 8, 128), F32)
+    out = pl.pallas_call(
         functools.partial(main_kernel, devices),
-        out_shape=(shaped(B, S, ROWS, FACE), shaped(B, ROWS, FACE)),
-        in_specs=[HBM] * 2 + [ANY] * 3 + [VMEM, VMEM] + [HBM] * 4,
-        out_specs=(HBM, HBM),
+        out_shape=(shaped(B, S, ROWS, FACE), shaped(B, ROWS, FACE), state),
+        in_specs=[VMEM] * 4 + [HBM] * 4,
+        out_specs=(HBM, HBM, VMEM),
         scratch_shapes=[
-            pltpu.VMEM((B, S, NT, H, 128), F32),
-            pltpu.VMEM((B, NT, H, 128), F32),
-            pltpu.VMEM((B, NT, H, 128), F32),
-            pltpu.VMEM((8, NT, 16, 128), F32),
-            pltpu.VMEM((NI, NT, 8, 128), F32),
-            pltpu.VMEM((NI, NT, 8, 128), F32),
+            link,
+            link,
             pltpu.VMEM((NI, NT, 8, 128), F32),
             pltpu.VMEM((8, 128), F32),
             *tables(devices),
             pltpu.SMEM((4,), F32),
             pltpu.SemaphoreType.DMA((B,)),
-            pltpu.SemaphoreType.DMA((3,)),
-            pltpu.SemaphoreType.DMA((B,)),
             pltpu.SemaphoreType.DMA((4,)),
         ],
+        input_output_aliases={0: 2},
         compiler_params=limit(40),
         name="transport",
-    )(
-        concentration, potential_guess, strips, got_e, got_o, w2, w_other,
-        block_rows, block_home, face_match, diffusivity,
-    )
+    )(x, w2, w_other, got_o, block_rows, block_home, face_match, diffusivity)
+    return out[0], out[1]
 
 
 def solution(mesh):

time: 45.7 us -> 43.9 us (0.961)
  waiting for transfers between devices: 5.43 us -> 4.44 us
    pallas_call x1, Pallas kernels: 9 us -> 7.37 us  [body(): pl.pallas_call(functools.partial(main_kernel, devices), out_shape=(shaped...]
    pallas_call x1 -> x5, Pallas kernels: 2.69 us -> 3.9 us  [the longest x1 2.53 us: body(): pl.pallas_call(functools.partial(pack_kernel, devices), out_shape=(messag...]
    ppermute x5, waiting for transfers between devices: 5.43 us -> 4.44 us  [swap(): return lax.ppermute(x, AXIS, pairs)]
  transfers between devices with their start and end apart: 5 -> 5, of which waited for: 4 -> 3; matrix products, arithmetic and copies ran while one was open for 1% -> 0% of each run, Pallas kernels for 0% -> 3%
where the time goes in v3:
time: 43.9 us; the launch traced here: 43.5 us
  starting transfers between devices  27.1 us (62%)
  Pallas kernels  11.3 us (26%)
  waiting for transfers between devices  4.44 us (10%)
  between operations  0.7 us (2%)
    ppermute x5, starting transfers between devices, swap(): return lax.ppermute(x, AXIS, pairs)  27.1 us
    pallas_call x1, Pallas kernels, body(): pl.pallas_call(functools.partial(main_kernel, devices), out_shape=(shaped...  7.37 us
    ppermute x5, waiting for transfers between devices, swap(): return lax.ppermute(x, AXIS, pairs)  4.44 us
    pallas_call x1, Pallas kernels, body(): pl.pallas_call(functools.partial(pack_kernel, devices), out_shape=(messag...  2.53 us
    pallas_call x1, Pallas kernels, body(): pl.pallas_call(functools.partial(prep_kernel, devices), out_shape=state,...  1.28 us
  transfers between devices with their start and end apart: 5, of which 3 were waited for; matrix products, arithmetic and copies ran while one was open for 0% of the time, Pallas kernels for 3%

profile of v3, /device:TPU:1, one launch (start us, length us, event | category | flops | bytes accessed | tf_op | source)
XLA Modules:
  0.0 43.5 jit_solution(3485789168606564814)
XLA Ops:
  0.6 2.5 %pack.1 = (f32[9,16,128]{2,1,0:T(8,128)S(1)}, f32[9,16,128]{2,1,0:T(8,128)S(1)}, f32[3,8,8,56,128]{4,3,2,1,0:T(8,128)S(1)}) custom-call(f32[3,4,40,1024]{3,2,1,0:T(8,128)} %conc.1, f32[3,40,1024]{2,1,0:T(8,128)} %pot.1, s32[3]{0:T(128)} %rows.5, s32[1536]{0:T(1024)} %home.5, s32[3,2,3]{2,1,0:T(2,128)} %match.5), custom_call_target="tpu_custom_call" | custom-call | tf_op jit(solution)/shard_map/pack/pallas_call | solution.py:477
  3.2 9.0 %collective-permute-start = (f32[9,16,128]{2,1,0:T(8,128)S(1)}, f32[9,16,128]{2,1,0:T(8,128)S(1)}, u32[]{:S(2)}, u32[]{:S(2)}) collective-permute-start(f32[9,16,128]{2,1,0:T(8,128)S(1)} %get-tuple-element.10), channel_id=1, source_target_pairs={{0,1},{1,0},{2,3},{3,2},{4,5},{5,4},{6,7},{7,6},{8,9},{9,8},{10,11... | collective-permute-start | bytes 221192 | tf_op jit(solution)/shard_map/ppermute | solution.py:467
  12.2 0.9 %collective-permute-done.got_e = f32[9,16,128]{2,1,0:T(8,128)S(1)} collective-permute-done((f32[9,16,128]{2,1,0:T(8,128)S(1)}, f32[9,16,128]{2,1,0:T(8,128)S(1)}, u32[]{:S(2)}, u32[]{:S(2)}) %collective-permute-start) | collective-permute-done | bytes 73760 | tf_op jit(solution)/shard_map/ppermute | solution.py:467
  13.1 10.2 %collective-permute-start.2 = (f32[152,128]{1,0:T(8,128)S(1)}, f32[152,128]{1,0:T(8,128)S(1)}, u32[]{:S(2)}, u32[]{:S(2)}) collective-permute-start(f32[152,128]{1,0:T(8,128)S(1)} %chip.1), channel_id=1, source_target_pairs={{506,0},{7,1},{508,2},{9,3},{510,4},{11,5},{0,6},{13,7},{2,8},{15,... | collective-permute-start | bytes 233480 | tf_op jit(solution)/shard_map/ppermute | solution.py:467
  23.3 1.9 %collective-permute-start.1 = (f32[152,128]{1,0:T(8,128)S(1)}, f32[152,128]{1,0:T(8,128)S(1)}, u32[]{:S(2)}, u32[]{:S(2)}) collective-permute-start(f32[152,128]{1,0:T(8,128)S(1)} %chip.1), channel_id=1, source_target_pairs={{508,0},{5,1},{510,2},{7,3},{0,4},{9,5},{2,6},{11,7},{4,8},{13,9},... | collective-permute-start | bytes 233480 | tf_op jit(solution)/shard_map/ppermute | solution.py:467
  25.2 1.9 %collective-permute-start.3 = (f32[9,16,128]{2,1,0:T(8,128)S(1)}, f32[9,16,128]{2,1,0:T(8,128)S(1)}, u32[]{:S(2)}, u32[]{:S(2)}) collective-permute-start(f32[9,16,128]{2,1,0:T(8,128)S(1)} %stamp.1), channel_id=1, source_target_pairs={{0,511},{1,2},{2,1},{3,4},{4,3},{5,6},{6,5},{7,8},{8,7},{9,10},{10... | collective-permute-start | bytes 221192 | tf_op jit(solution)/shard_map/ppermute | solution.py:467
  27.2 1.3 %prep.1._ = f32[3,8,8,56,128]{4,3,2,1,0:T(8,128)S(1)} custom-call(f32[3,8,8,56,128]{4,3,2,1,0:T(8,128)S(1)} %get-tuple-element.9._, f32[9,16,128]{2,1,0:T(8,128)S(1)} %collective-permute-done.got_e, s32[3]{0:T(128)} %rows.5, s32[1536]{0:T(1024)} %home.5, s32[3,2,3]{2,1,0:T(2,128)} %match.5), custom_call_target="tpu_custom_call", output_to_operand_aliasing={{}: (0, {})} | custom-call | tf_op jit(solution)/shard_map/prep/pallas_call | solution.py:512
  28.5 2.7 %collective-permute-done.3.got_o = f32[9,16,128]{2,1,0:T(8,128)S(1)} collective-permute-done((f32[9,16,128]{2,1,0:T(8,128)S(1)}, f32[9,16,128]{2,1,0:T(8,128)S(1)}, u32[]{:S(2)}, u32[]{:S(2)}) %collective-permute-start.3) | collective-permute-done | bytes 73760 | tf_op jit(solution)/shard_map/ppermute | solution.py:467
  31.2 0.0 collective-permute-done.2.third
  31.2 0.0 collective-permute-done.1.second
  31.2 0.1 join.1.w_mine
  31.3 4.0 %collective-permute-start.4 = (f32[8,128]{1,0:T(8,128)S(1)}, f32[8,128]{1,0:T(8,128)S(1)}, u32[]{:S(2)}, u32[]{:S(2)}) collective-permute-start(f32[8,128]{1,0:T(8,128)S(1)} %join.1.w_mine), channel_id=1, source_target_pairs={{0,1},{1,0},{2,3},{3,2},{4,5},{5,4},{6,7},{7,6},{8,9},{9,8},{10,11... | collective-permute-start | bytes 12296 | tf_op jit(solution)/shard_map/ppermute | solution.py:467
  35.3 0.8 %collective-permute-done.4.w_theirs = f32[8,128]{1,0:T(8,128)S(1)} collective-permute-done((f32[8,128]{1,0:T(8,128)S(1)}, f32[8,128]{1,0:T(8,128)S(1)}, u32[]{:S(2)}, u32[]{:S(2)}) %collective-permute-start.4) | collective-permute-done | bytes 4128 | tf_op jit(solution)/shard_map/ppermute | solution.py:467
  36.1 7.4 %transport.1 = (f32[3,4,40,1024]{3,2,1,0:T(8,128)}, f32[3,40,1024]{2,1,0:T(8,128)}, f32[3,8,8,56,128]{4,3,2,1,0:T(8,128)S(1)}) custom-call(f32[3,8,8,56,128]{4,3,2,1,0:T(8,128)S(1)} %prep.1._, f32[8,128]{1,0:T(8,128)S(1)} %join.1.w_mine, f32[8,128]{1,0:T(8,128)S(1)} %collective-permute-done.4.w_theirs, ...), custom_call_target="tpu_custom_call", output_to_operand_aliasing={{2}: (0, {})} | custom-call | tf_op jit(solution)/shard_map/transport/pallas_call | solution.py:535
  (2 shorter events, 0.0 us)
Async XLA Ops:
  3.2 9.9 %collective-permute-start = (f32[9,16,128]{2,1,0:T(8,128)S(1)}, f32[9,16,128]{2,1,0:T(8,128)S(1)}, u32[]{:S(2)}, u32[]{:S(2)}) collective-permute-start(f32[9,16,128]{2,1,0:T(8,128)S(1)} %get-tuple-element.10), channel_id=1, source_target_pairs={{0,1},{1,0},{2,3},{3,2},{4,5},{5,4},{6,7},{7,6},{8,9},{9,8},{10,11... | collective-permute-start | bytes 221192 | tf_op jit(solution)/shard_map/ppermute | solution.py:467
  13.1 18.1 %collective-permute-start.2 = (f32[152,128]{1,0:T(8,128)S(1)}, f32[152,128]{1,0:T(8,128)S(1)}, u32[]{:S(2)}, u32[]{:S(2)}) collective-permute-start(f32[152,128]{1,0:T(8,128)S(1)} %chip.1), channel_id=1, source_target_pairs={{506,0},{7,1},{508,2},{9,3},{510,4},{11,5},{0,6},{13,7},{2,8},{15,... | collective-permute-start | bytes 233480 | tf_op jit(solution)/shard_map/ppermute | solution.py:467
  23.3 7.9 %collective-permute-start.1 = (f32[152,128]{1,0:T(8,128)S(1)}, f32[152,128]{1,0:T(8,128)S(1)}, u32[]{:S(2)}, u32[]{:S(2)}) collective-permute-start(f32[152,128]{1,0:T(8,128)S(1)} %chip.1), channel_id=1, source_target_pairs={{508,0},{5,1},{510,2},{7,3},{0,4},{9,5},{2,6},{11,7},{4,8},{13,9},... | collective-permute-start | bytes 233480 | tf_op jit(solution)/shard_map/ppermute | solution.py:467
  25.2 6.0 %collective-permute-start.3 = (f32[9,16,128]{2,1,0:T(8,128)S(1)}, f32[9,16,128]{2,1,0:T(8,128)S(1)}, u32[]{:S(2)}, u32[]{:S(2)}) collective-permute-start(f32[9,16,128]{2,1,0:T(8,128)S(1)} %stamp.1), channel_id=1, source_target_pairs={{0,511},{1,2},{2,1},{3,4},{4,3},{5,6},{6,5},{7,8},{8,7},{9,10},{10... | collective-permute-start | bytes 221192 | tf_op jit(solution)/shard_map/ppermute | solution.py:467
  31.3 4.8 %collective-permute-start.4 = (f32[8,128]{1,0:T(8,128)S(1)}, f32[8,128]{1,0:T(8,128)S(1)}, u32[]{:S(2)}, u32[]{:S(2)}) collective-permute-start(f32[8,128]{1,0:T(8,128)S(1)} %join.1.w_mine), channel_id=1, source_target_pairs={{0,1},{1,0},{2,3},{3,2},{4,5},{5,4},{6,7},{7,6},{8,9},{9,8},{10,11... | collective-permute-start | bytes 12296 | tf_op jit(solution)/shard_map/ppermute | solution.py:467

commit v4 on v3

--- a/solution.py
+++ b/solution.py
@@ -14,6 +14,7 @@
 H = 56
 NI = 6
 VALENCES = (1.0, -1.0, 2.0, -1.0)
+GUESS, CHARGE, STRIP, LEFT, RIGHT, WIDE, PLANES = 4, 5, 6, 8, 12, 16, 17
 FAR = 152
 W_IN, W_EDGE = 0.8 / 4.5, 0.8 / 3.5
 WALL = -1000.0
@@ -211,6 +212,16 @@
     return g_row + jnp.sum(m_row * x, axis=0, keepdims=True)
 
 
+def shift_right(tiles, last):
+    moved = [pltpu.roll(t, 127, 1) for t in tiles] + [jnp.zeros_like(tiles[0])]
+    return [jnp.where(last, moved[j + 1], moved[j]) for j in range(NT)]
+
+
+def shift_left(tiles, first):
+    moved = [jnp.zeros_like(tiles[0])] + [pltpu.roll(t, 1, 1) for t in tiles]
+    return [jnp.where(first, moved[j], moved[j + 1]) for j in range(NT)]
+
+
 def insert(U, G, Q, b, side, n, strip):
     for k in range(4):
         row = pl.ds(LO - 1 - k if side == 0 else LO + n + k, 1)
@@ -234,6 +245,7 @@
         c.wait()
     rowid = iota((ROWS, 128), 0)
     zero = jnp.zeros((8, 128), F32)
+    first, last = iota((8, 128), 1) == 0, iota((8, 128), 1) == 127
 
     def block(b, _):
         n = rows_s[b]
@@ -256,6 +268,22 @@
             def _():
                 insert(U, G, Q, b, side, n, got_e)
 
+        for i in range(NI):
+            at = pl.ds(4 + i, 8, stride=NI)
+            g = [X[b, GUESS, j, at, :] for j in range(NT)]
+            for j, (x, y) in enumerate(zip(shift_left(g, first), shift_right(g, last))):
+                X[b, WIDE, j, at, :] = X[b, CHARGE, j, at, :] + (x + y)
+
+        def species(s, _):
+            for i in range(NI):
+                at = pl.ds(4 + i, 8, stride=NI)
+                u = [X[b, s, j, at, :] for j in range(NT)]
+                for j, (x, y) in enumerate(zip(shift_left(u, first), shift_right(u, last))):
+                    X[b, LEFT + s, j, at, :] = x
+                    X[b, RIGHT + s, j, at, :] = y
+            return 0
+
+        lax.fori_loop(0, S, species, 0, unroll=True)
         return 0
 
     lax.fori_loop(0, B, block, 0)
@@ -263,7 +291,7 @@
 
 def main_kernel(
     devices, _, w_mine, w_theirs, got_o, rows, home, match, diff,
-    end_out, pot_out, X, LV, LH, MIDS, CR, rows_s, home_s, match_s, diff_s, out_sem, tab_sem,
+    end_out, pot_out, X, LV, LH, MIDS, CR, SL, SR, rows_s, home_s, match_s, diff_s, out_sem, tab_sem,
 ):
     me = lax.axis_index(AXIS)
     core = lax.rem(me, 2)
@@ -294,10 +322,15 @@
     in_chip = (l8 >= MID) & (l8 < MID + 6)
     W = w_mine[...] + jnp.where(in_chip, 0.0, w_theirs[...])
     CR[...] = jnp.broadcast_to(coarse(W), (8, 128))
+    first, last = l8 == 0, l8 == 127
+    for h in range(0, 16, 8):
+        strip = [got_o[j, h : h + 8, :] for j in range(NT)]
+        for j, (x, y) in enumerate(zip(shift_left(strip, first), shift_right(strip, last))):
+            SL[j, h : h + 8, :] = x
+            SR[j, h : h + 8, :] = y
     for c in loads:
         c.wait()
 
-    first, last = l8 == 0, l8 == 127
     zero = jnp.zeros((8, 128), F32)
 
     def at(i):
@@ -329,6 +362,15 @@
             @pl.when(info[side][0] & (info[side][1] == 2 * core))
             def _():
                 insert(U, G, Q, b, side, n, got_o)
+                for k in range(3):
+                    row = pl.ds(LO - 1 - k if side == 0 else LO + n + k, 1)
+                    sides = SL[:, k : k + 1, :] + SR[:, k : k + 1, :]
+                    X[b, WIDE, :, row, :] = got_o[0:NT, 4 + k : 5 + k, :] + sides
+                    if k < 2:
+                        for s in range(S):
+                            m = 7 + 2 * s + k
+                            X[b, LEFT + s, :, row, :] = SL[:, m : m + 1, :]
+                            X[b, RIGHT + s, :, row, :] = SR[:, m : m + 1, :]
 
         lane_own = MID + B * core + b
         cr = CR[...]
@@ -360,44 +402,45 @@
                 return jnp.where(last, w_edge[i], w_in[i])
             return w_in[i]
 
-        def smooth(load, store):
-            prv, cur = None, [load(i, 0) for i in range(NI)]
-            for j in range(NT):
-                nxt = [load(i, j + 1) for i in range(NI)] if j < NT - 1 else None
-                u, d, lf, rt = up(cur), down(cur), left_of(cur, prv), right_of(cur, nxt)
-                for i in range(NI):
-                    q = Q[b, j, at(i), :]
-                    store(i, j, 0.2 * cur[i] + weight(i, j) * (q + ((u[i] + d[i]) + (lf[i] + rt[i]))))
-                prv, cur = cur, nxt
-
-        def put_v(i, j, x):
-            MIDS[i, j] = x + corr[i]
-
-        def put_phi(i, j, x):
-            G[b, j, at(i), :] = jnp.where(alive[i], x, 0.0)
-            LV[0, i, j] = x
-
-        smooth(lambda i, j: G[b, j, at(i), :], put_v)
-        smooth(lambda i, j: MIDS[i, j], put_phi)
+        for j in range(NT):
+            cur = [G[b, j, at(i), :] for i in range(NI)]
+            u, d = up(cur), down(cur)
+            for i in range(NI):
+                x = 0.2 * cur[i] + weight(i, j) * (X[b, WIDE, j, at(i), :] + (u[i] + d[i]))
+                MIDS[i, j] = x + corr[i]
+        prv, cur = None, [MIDS[i, 0] for i in range(NI)]
+        for j in range(NT):
+            nxt = [MIDS[i, j + 1] for i in range(NI)] if j < NT - 1 else None
+            u, d, lf, rt = up(cur), down(cur), left_of(cur, prv), right_of(cur, nxt)
+            for i in range(NI):
+                q = Q[b, j, at(i), :]
+                x = 0.2 * cur[i] + weight(i, j) * (q + ((u[i] + d[i]) + (lf[i] + rt[i])))
+                G[b, j, at(i), :] = jnp.where(alive[i], x, 0.0)
+                LV[0, i, j] = x
+            prv, cur = cur, nxt
         for c in pot_copies(b):
             c.start()
 
-        def factors(ref, i, j, mask, step):
-            half = step * (0.5 * mask)
-            a, d = mask + half, mask - half
-            ref[0, i, j], ref[1, i, j] = a, d
-            ref[2, i, j], ref[3, i, j] = a + half, d - half
-
         one = jnp.ones((8, 128), F32)
-        wall_right = jnp.where(last, 0.0, one)
-        cur = [LV[0, i, 0] for i in range(NI)]
+        edge_right, edge_left = jnp.where(last, 0.0, one), jnp.where(first, 0.0, one)
+        prv, cur = None, [LV[0, i, 0] for i in range(NI)]
         for j in range(NT):
             nxt = [LV[0, i, j + 1] for i in range(NI)] if j < NT - 1 else None
             u, rt = up(cur), right_of(cur, nxt)
+            m = edge_right if j == NT - 1 else one
+            ml = edge_left if j == 0 else one
+            step = [(0.5 * m) * (rt[i] - cur[i]) for i in range(NI)]
+            past = left_of(step, prv)
             for i in range(NI):
-                factors(LV, i, j, linked[i], u[i] - cur[i])
-                factors(LH, i, j, wall_right if j == NT - 1 else one, rt[i] - cur[i])
-            cur = nxt
+                half = (0.5 * linked[i]) * (u[i] - cur[i])
+                a, d = linked[i] + half, linked[i] - half
+                LV[0, i, j], LV[1, i, j], LV[2, i, j], LV[3, i, j] = a, d, a + half, d - half
+                a, d, al, dl = m + step[i], m - step[i], ml + past[i], ml - past[i]
+                LH[0, i, j], LH[1, i, j], LH[2, i, j] = a, dl, d + al
+                LH[3, i, j], LH[4, i, j], LH[5, i, j] = d, al, a + dl
+                LH[6, i, j], LH[7, i, j] = a + step[i], dl - past[i]
+                LH[8, i, j] = (d - step[i]) + (al + past[i])
+            prv, cur = step, nxt
 
         def species(s, _):
             ia = jnp.where(s == 0, 0, jnp.where(s == 2, 2, 1))
@@ -405,32 +448,36 @@
             k1 = 0.1 * diff_s[s]
             k2 = 0.05 * diff_s[s]
 
-            def stage(load, store):
-                prv, cur = None, [load(i, 0) for i in range(NI)]
-                for j in range(NT):
-                    nxt = [load(i, j + 1) for i in range(NI)] if j < NT - 1 else None
-                    u, rt = up(cur), right_of(cur, nxt)
-                    fv = [u[i] * LV[ia, i, j] - cur[i] * LV[ib, i, j] for i in range(NI)]
-                    fh = [rt[i] * LH[ia, i, j] - cur[i] * LH[ib, i, j] for i in range(NI)]
-                    fd, fl = down(fv), left_of(fh, prv)
-                    for i in range(NI):
-                        store(i, j, cur[i], (fv[i] - fd[i]) + (fh[i] - fl[i]))
-                    prv, cur = fh, nxt
-
-            def put_mid(i, j, u, rate):
-                MIDS[i, j] = u + k1 * rate
-
-            def put_end(i, j, mid, rate):
-                x = 0.5 * (U[b, s, j, at(i), :] + mid) + k2 * rate
-                U[b, s, j, at(i), :] = jnp.where(alive[i], x, 0.0)
-
-            stage(lambda i, j: U[b, s, j, at(i), :], put_mid)
-            stage(lambda i, j: MIDS[i, j], put_end)
+            ih = jnp.where(s == 0, 0, jnp.where(s == 2, 6, 3))
+
+            def rates(j, cur, lf, rt):
+                u = up(cur)
+                fv = [u[i] * LV[ia, i, j] - cur[i] * LV[ib, i, j] for i in range(NI)]
+                fd = down(fv)
+                fh = [
+                    (rt[i] * LH[ih, i, j] + lf[i] * LH[ih + 1, i, j]) - cur[i] * LH[ih + 2, i, j]
+                    for i in range(NI)
+                ]
+                return [(fv[i] - fd[i]) + fh[i] for i in range(NI)]
+
+            for j in range(NT):
+                cur, lf, rt = ([X[b, p + s, j, at(i), :] for i in range(NI)] for p in (0, LEFT, RIGHT))
+                rate = rates(j, cur, lf, rt)
+                for i in range(NI):
+                    MIDS[i, j] = cur[i] + k1 * rate[i]
+            prv, cur = None, [MIDS[i, 0] for i in range(NI)]
+            for j in range(NT):
+                nxt = [MIDS[i, j + 1] for i in range(NI)] if j < NT - 1 else None
+                rate = rates(j, cur, left_of(cur, prv), right_of(cur, nxt))
+                for i in range(NI):
+                    x = 0.5 * (U[b, s, j, at(i), :] + cur[i]) + k2 * rate[i]
+                    U[b, s, j, at(i), :] = jnp.where(alive[i], x, 0.0)
+                prv, cur = cur, nxt
             for c in end_copies(b, s):
                 c.start()
             return 0
 
-        lax.fori_loop(0, S, species, 0)
+        lax.fori_loop(0, S, species, 0, unroll=True)
         return 0
 
     lax.fori_loop(0, B, block, 0)
@@ -472,7 +519,7 @@
         return [((i + k if i % 2 else i - k) % devices, i) for i in range(devices)]
 
 
-    state = pltpu.VMEM((B, S + 4, NT, H, 128), F32)
+    state = pltpu.VMEM((B, PLANES, NT, H, 128), F32)
     message = pltpu.VMEM((NT + 1, 16, 128), F32)
     msg_e, msg_o, x = pl.pallas_call(
         functools.partial(pack_kernel, devices),
@@ -531,17 +578,18 @@
     )(chip, second, third, got_o)
     w_other = swap(w2, on_chip)
 
-    link = pltpu.VMEM((4, NI, NT, 8, 128), F32)
     out = pl.pallas_call(
         functools.partial(main_kernel, devices),
         out_shape=(shaped(B, S, ROWS, FACE), shaped(B, ROWS, FACE), state),
         in_specs=[VMEM] * 4 + [HBM] * 4,
         out_specs=(HBM, HBM, VMEM),
         scratch_shapes=[
-            link,
-            link,
+            pltpu.VMEM((4, NI, NT, 8, 128), F32),
+            pltpu.VMEM((9, NI, NT, 8, 128), F32),
             pltpu.VMEM((NI, NT, 8, 128), F32),
             pltpu.VMEM((8, 128), F32),
+            pltpu.VMEM((NT, 16, 128), F32),
+            pltpu.VMEM((NT, 16, 128), F32),
             *tables(devices),
             pltpu.SMEM((4,), F32),
             pltpu.SemaphoreType.DMA((B,)),

time: 43.9 us -> 42.3 us (0.964)
  waiting for transfers between devices: 4.44 us -> 2.74 us
    pallas_call x1, Pallas kernels: 1.28 us -> 2.98 us  [body(): pl.pallas_call(functools.partial(prep_kernel, devices), out_shape=state,...]
    ppermute x5, waiting for transfers between devices: 4.44 us -> 2.74 us  [swap(): return lax.ppermute(x, AXIS, pairs)]
    pallas_call x1, Pallas kernels: 7.37 us -> 5.86 us  [body(): pl.pallas_call(functools.partial(main_kernel, devices), out_shape=(shaped...]
  transfers between devices with their start and end apart: 5 -> 5, of which waited for: 3 -> 3; matrix products, arithmetic and copies ran while one was open for 0% -> 0% of each run, Pallas kernels for 3% -> 7%
where the time goes in v4:
time: 42.3 us; the launch traced here: 42 us
  starting transfers between devices  27 us (64%)
  Pallas kernels  11.5 us (27%)
  waiting for transfers between devices  2.74 us (6%)
  between operations  0.7 us (2%)
    ppermute x5, starting transfers between devices, swap(): return lax.ppermute(x, AXIS, pairs)  27 us
    pallas_call x1, Pallas kernels, body(): pl.pallas_call(functools.partial(main_kernel, devices), out_shape=(shaped...  5.86 us
    pallas_call x1, Pallas kernels, body(): pl.pallas_call(functools.partial(prep_kernel, devices), out_shape=state,...  2.98 us
    ppermute x5, waiting for transfers between devices, swap(): return lax.ppermute(x, AXIS, pairs)  2.74 us
    pallas_call x1, Pallas kernels, body(): pl.pallas_call(functools.partial(pack_kernel, devices), out_shape=(messag...  2.62 us
  transfers between devices with their start and end apart: 5, of which 3 were waited for; matrix products, arithmetic and copies ran while one was open for 0% of the time, Pallas kernels for 7%

profile of v4, /device:TPU:1, one launch (start us, length us, event | category | flops | bytes accessed | tf_op | source)
XLA Modules:
  0.0 42.0 jit_solution(10458260011433989261)
XLA Ops:
  0.6 2.6 %pack.1 = (f32[9,16,128]{2,1,0:T(8,128)S(1)}, f32[9,16,128]{2,1,0:T(8,128)S(1)}, f32[3,17,8,56,128]{4,3,2,1,0:T(8,128)S(1)}) custom-call(f32[3,4,40,1024]{3,2,1,0:T(8,128)} %conc.1, f32[3,40,1024]{2,1,0:T(8,128)} %pot.1, s32[3]{0:T(128)} %rows.5, s32[1536]{0:T(1024)} %home.5, s32[3,2,3]{2,1,0:T(2,128)} %match.5), custom_call_target="tpu_custom_call" | custom-call | tf_op jit(solution)/shard_map/pack/pallas_call | solution.py:524
  3.3 8.7 %collective-permute-start = (f32[9,16,128]{2,1,0:T(8,128)S(1)}, f32[9,16,128]{2,1,0:T(8,128)S(1)}, u32[]{:S(2)}, u32[]{:S(2)}) collective-permute-start(f32[9,16,128]{2,1,0:T(8,128)S(1)} %get-tuple-element.10), channel_id=1, source_target_pairs={{0,1},{1,0},{2,3},{3,2},{4,5},{5,4},{6,7},{7,6},{8,9},{9,8},{10,11... | collective-permute-start | bytes 221192 | tf_op jit(solution)/shard_map/ppermute | solution.py:514
  11.9 0.9 %collective-permute-done.got_e = f32[9,16,128]{2,1,0:T(8,128)S(1)} collective-permute-done((f32[9,16,128]{2,1,0:T(8,128)S(1)}, f32[9,16,128]{2,1,0:T(8,128)S(1)}, u32[]{:S(2)}, u32[]{:S(2)}) %collective-permute-start) | collective-permute-done | bytes 73760 | tf_op jit(solution)/shard_map/ppermute | solution.py:514
  12.8 10.4 %collective-permute-start.2 = (f32[152,128]{1,0:T(8,128)S(1)}, f32[152,128]{1,0:T(8,128)S(1)}, u32[]{:S(2)}, u32[]{:S(2)}) collective-permute-start(f32[152,128]{1,0:T(8,128)S(1)} %chip.1), channel_id=1, source_target_pairs={{506,0},{7,1},{508,2},{9,3},{510,4},{11,5},{0,6},{13,7},{2,8},{15,... | collective-permute-start | bytes 233480 | tf_op jit(solution)/shard_map/ppermute | solution.py:514
  23.3 2.0 %collective-permute-start.1 = (f32[152,128]{1,0:T(8,128)S(1)}, f32[152,128]{1,0:T(8,128)S(1)}, u32[]{:S(2)}, u32[]{:S(2)}) collective-permute-start(f32[152,128]{1,0:T(8,128)S(1)} %chip.1), channel_id=1, source_target_pairs={{508,0},{5,1},{510,2},{7,3},{0,4},{9,5},{2,6},{11,7},{4,8},{13,9},... | collective-permute-start | bytes 233480 | tf_op jit(solution)/shard_map/ppermute | solution.py:514
  25.3 1.9 %collective-permute-start.3 = (f32[9,16,128]{2,1,0:T(8,128)S(1)}, f32[9,16,128]{2,1,0:T(8,128)S(1)}, u32[]{:S(2)}, u32[]{:S(2)}) collective-permute-start(f32[9,16,128]{2,1,0:T(8,128)S(1)} %stamp.1), channel_id=1, source_target_pairs={{0,511},{1,2},{2,1},{3,4},{4,3},{5,6},{6,5},{7,8},{8,7},{9,10},{10... | collective-permute-start | bytes 221192 | tf_op jit(solution)/shard_map/ppermute | solution.py:514
  27.2 3.0 %prep.1._ = f32[3,17,8,56,128]{4,3,2,1,0:T(8,128)S(1)} custom-call(f32[3,17,8,56,128]{4,3,2,1,0:T(8,128)S(1)} %get-tuple-element.9._, f32[9,16,128]{2,1,0:T(8,128)S(1)} %collective-permute-done.got_e, s32[3]{0:T(128)} %rows.5, s32[1536]{0:T(1024)} %home.5, s32[3,2,3]{2,1,0:T(2,128)} %match.5), custom_call_target="tpu_custom_call", output_to_operand_aliasing={{}: (0, {})} | custom-call | tf_op jit(solution)/shard_map/prep/pallas_call | solution.py:559
  30.2 1.0 %collective-permute-done.3.got_o = f32[9,16,128]{2,1,0:T(8,128)S(1)} collective-permute-done((f32[9,16,128]{2,1,0:T(8,128)S(1)}, f32[9,16,128]{2,1,0:T(8,128)S(1)}, u32[]{:S(2)}, u32[]{:S(2)}) %collective-permute-start.3) | collective-permute-done | bytes 73760 | tf_op jit(solution)/shard_map/ppermute | solution.py:514
  31.2 0.0 collective-permute-done.2.third
  31.2 0.0 collective-permute-done.1.second
  31.2 0.1 join.1.w_mine
  31.3 4.0 %collective-permute-start.4 = (f32[8,128]{1,0:T(8,128)S(1)}, f32[8,128]{1,0:T(8,128)S(1)}, u32[]{:S(2)}, u32[]{:S(2)}) collective-permute-start(f32[8,128]{1,0:T(8,128)S(1)} %join.1.w_mine), channel_id=1, source_target_pairs={{0,1},{1,0},{2,3},{3,2},{4,5},{5,4},{6,7},{7,6},{8,9},{9,8},{10,11... | collective-permute-start | bytes 12296 | tf_op jit(solution)/shard_map/ppermute | solution.py:514
  35.3 0.8 %collective-permute-done.4.w_theirs = f32[8,128]{1,0:T(8,128)S(1)} collective-permute-done((f32[8,128]{1,0:T(8,128)S(1)}, f32[8,128]{1,0:T(8,128)S(1)}, u32[]{:S(2)}, u32[]{:S(2)}) %collective-permute-start.4) | collective-permute-done | bytes 4128 | tf_op jit(solution)/shard_map/ppermute | solution.py:514
  36.1 5.9 %transport.1 = (f32[3,4,40,1024]{3,2,1,0:T(8,128)}, f32[3,40,1024]{2,1,0:T(8,128)}, f32[3,17,8,56,128]{4,3,2,1,0:T(8,128)S(1)}) custom-call(f32[3,17,8,56,128]{4,3,2,1,0:T(8,128)S(1)} %prep.1._, f32[8,128]{1,0:T(8,128)S(1)} %join.1.w_mine, f32[8,128]{1,0:T(8,128)S(1)} %collective-permute-done.4.w_theirs, ...), custom_call_target="tpu_custom_call", output_to_operand_aliasing={{2}: (0, {})} | custom-call | tf_op jit(solution)/shard_map/transport/pallas_call | solution.py:581
  (2 shorter events, 0.0 us)
Async XLA Ops:
  3.3 9.6 %collective-permute-start = (f32[9,16,128]{2,1,0:T(8,128)S(1)}, f32[9,16,128]{2,1,0:T(8,128)S(1)}, u32[]{:S(2)}, u32[]{:S(2)}) collective-permute-start(f32[9,16,128]{2,1,0:T(8,128)S(1)} %get-tuple-element.10), channel_id=1, source_target_pairs={{0,1},{1,0},{2,3},{3,2},{4,5},{5,4},{6,7},{7,6},{8,9},{9,8},{10,11... | collective-permute-start | bytes 221192 | tf_op jit(solution)/shard_map/ppermute | solution.py:514
  12.8 18.4 %collective-permute-start.2 = (f32[152,128]{1,0:T(8,128)S(1)}, f32[152,128]{1,0:T(8,128)S(1)}, u32[]{:S(2)}, u32[]{:S(2)}) collective-permute-start(f32[152,128]{1,0:T(8,128)S(1)} %chip.1), channel_id=1, source_target_pairs={{506,0},{7,1},{508,2},{9,3},{510,4},{11,5},{0,6},{13,7},{2,8},{15,... | collective-permute-start | bytes 233480 | tf_op jit(solution)/shard_map/ppermute | solution.py:514
  23.3 8.0 %collective-permute-start.1 = (f32[152,128]{1,0:T(8,128)S(1)}, f32[152,128]{1,0:T(8,128)S(1)}, u32[]{:S(2)}, u32[]{:S(2)}) collective-permute-start(f32[152,128]{1,0:T(8,128)S(1)} %chip.1), channel_id=1, source_target_pairs={{508,0},{5,1},{510,2},{7,3},{0,4},{9,5},{2,6},{11,7},{4,8},{13,9},... | collective-permute-start | bytes 233480 | tf_op jit(solution)/shard_map/ppermute | solution.py:514
  25.3 6.0 %collective-permute-start.3 = (f32[9,16,128]{2,1,0:T(8,128)S(1)}, f32[9,16,128]{2,1,0:T(8,128)S(1)}, u32[]{:S(2)}, u32[]{:S(2)}) collective-permute-start(f32[9,16,128]{2,1,0:T(8,128)S(1)} %stamp.1), channel_id=1, source_target_pairs={{0,511},{1,2},{2,1},{3,4},{4,3},{5,6},{6,5},{7,8},{8,7},{9,10},{10... | collective-permute-start | bytes 221192 | tf_op jit(solution)/shard_map/ppermute | solution.py:514
  31.3 4.8 %collective-permute-start.4 = (f32[8,128]{1,0:T(8,128)S(1)}, f32[8,128]{1,0:T(8,128)S(1)}, u32[]{:S(2)}, u32[]{:S(2)}) collective-permute-start(f32[8,128]{1,0:T(8,128)S(1)} %join.1.w_mine), channel_id=1, source_target_pairs={{0,1},{1,0},{2,3},{3,2},{4,5},{5,4},{6,7},{7,6},{8,9},{9,8},{10,11... | collective-permute-start | bytes 12296 | tf_op jit(solution)/shard_map/ppermute | solution.py:514

commit v5 on v4

--- a/solution.py
+++ b/solution.py
@@ -177,7 +177,7 @@
     msg_o[NT, 0:8, :] = chip[0:8, :]
 
 
-def join_kernel(chip, second, third, got_o, out):
+def join_kernel(chip, third, second, got_o, out):
     core = lax.rem(lax.axis_index(AXIS), 2)
     total = chip[0:8, :]
     for k, x in enumerate((got_o[NT, 0:8, :], second[0:8, :], third[0:8, :])):
@@ -575,7 +575,7 @@
         out_specs=VMEM,
         compiler_params=limit(1),
         name="join",
-    )(chip, second, third, got_o)
+    )(chip, third, second, got_o)
     w_other = swap(w2, on_chip)
 
     out = pl.pallas_call(

time: 42.3 us -> 42.4 us (level)
  no operation moved by 1% of the time
where the time goes in v5:
time: 42.4 us; the launch traced here: 42 us
  starting transfers between devices  26.9 us (63%)
  Pallas kernels  11.6 us (27%)
  waiting for transfers between devices  2.75 us (6%)
  between operations  0.7 us (2%)
    ppermute x5, starting transfers between devices, swap(): return lax.ppermute(x, AXIS, pairs)  26.9 us
    pallas_call x1, Pallas kernels, body(): pl.pallas_call(functools.partial(main_kernel, devices), out_shape=(shaped...  5.86 us
    pallas_call x1, Pallas kernels, body(): pl.pallas_call(functools.partial(prep_kernel, devices), out_shape=state,...  3.09 us
    ppermute x5, waiting for transfers between devices, swap(): return lax.ppermute(x, AXIS, pairs)  2.75 us
    pallas_call x1, Pallas kernels, body(): pl.pallas_call(functools.partial(pack_kernel, devices), out_shape=(messag...  2.61 us
  transfers between devices with their start and end apart: 5, of which 3 were waited for; matrix products, arithmetic and copies ran while one was open for 0% of the time, Pallas kernels for 7%

profile of v5, /device:TPU:1, one launch (start us, length us, event | category | flops | bytes accessed | tf_op | source)
XLA Modules:
  0.0 42.0 jit_solution(14276820205741339454)
XLA Ops:
  0.6 2.6 %pack.1 = (f32[9,16,128]{2,1,0:T(8,128)S(1)}, f32[9,16,128]{2,1,0:T(8,128)S(1)}, f32[3,17,8,56,128]{4,3,2,1,0:T(8,128)S(1)}) custom-call(f32[3,4,40,1024]{3,2,1,0:T(8,128)} %conc.1, f32[3,40,1024]{2,1,0:T(8,128)} %pot.1, s32[3]{0:T(128)} %rows.5, s32[1536]{0:T(1024)} %home.5, s32[3,2,3]{2,1,0:T(2,128)} %match.5), custom_call_target="tpu_custom_call" | custom-call | tf_op jit(solution)/shard_map/pack/pallas_call | solution.py:524
  3.2 8.8 %collective-permute-start = (f32[9,16,128]{2,1,0:T(8,128)S(1)}, f32[9,16,128]{2,1,0:T(8,128)S(1)}, u32[]{:S(2)}, u32[]{:S(2)}) collective-permute-start(f32[9,16,128]{2,1,0:T(8,128)S(1)} %get-tuple-element.10), channel_id=1, source_target_pairs={{0,1},{1,0},{2,3},{3,2},{4,5},{5,4},{6,7},{7,6},{8,9},{9,8},{10,11... | collective-permute-start | bytes 221192 | tf_op jit(solution)/shard_map/ppermute | solution.py:514
  12.0 0.9 %collective-permute-done.got_e = f32[9,16,128]{2,1,0:T(8,128)S(1)} collective-permute-done((f32[9,16,128]{2,1,0:T(8,128)S(1)}, f32[9,16,128]{2,1,0:T(8,128)S(1)}, u32[]{:S(2)}, u32[]{:S(2)}) %collective-permute-start) | collective-permute-done | bytes 73760 | tf_op jit(solution)/shard_map/ppermute | solution.py:514
  12.9 10.4 %collective-permute-start.2 = (f32[152,128]{1,0:T(8,128)S(1)}, f32[152,128]{1,0:T(8,128)S(1)}, u32[]{:S(2)}, u32[]{:S(2)}) collective-permute-start(f32[152,128]{1,0:T(8,128)S(1)} %chip.1), channel_id=1, source_target_pairs={{508,0},{5,1},{510,2},{7,3},{0,4},{9,5},{2,6},{11,7},{4,8},{13,9},... | collective-permute-start | bytes 233480 | tf_op jit(solution)/shard_map/ppermute | solution.py:514
  23.3 1.9 %collective-permute-start.1 = (f32[152,128]{1,0:T(8,128)S(1)}, f32[152,128]{1,0:T(8,128)S(1)}, u32[]{:S(2)}, u32[]{:S(2)}) collective-permute-start(f32[152,128]{1,0:T(8,128)S(1)} %chip.1), channel_id=1, source_target_pairs={{506,0},{7,1},{508,2},{9,3},{510,4},{11,5},{0,6},{13,7},{2,8},{15,... | collective-permute-start | bytes 233480 | tf_op jit(solution)/shard_map/ppermute | solution.py:514
  25.2 1.9 %collective-permute-start.3 = (f32[9,16,128]{2,1,0:T(8,128)S(1)}, f32[9,16,128]{2,1,0:T(8,128)S(1)}, u32[]{:S(2)}, u32[]{:S(2)}) collective-permute-start(f32[9,16,128]{2,1,0:T(8,128)S(1)} %stamp.1), channel_id=1, source_target_pairs={{0,511},{1,2},{2,1},{3,4},{4,3},{5,6},{6,5},{7,8},{8,7},{9,10},{10... | collective-permute-start | bytes 221192 | tf_op jit(solution)/shard_map/ppermute | solution.py:514
  27.2 3.1 %prep.1._ = f32[3,17,8,56,128]{4,3,2,1,0:T(8,128)S(1)} custom-call(f32[3,17,8,56,128]{4,3,2,1,0:T(8,128)S(1)} %get-tuple-element.9._, f32[9,16,128]{2,1,0:T(8,128)S(1)} %collective-permute-done.got_e, s32[3]{0:T(128)} %rows.5, s32[1536]{0:T(1024)} %home.5, s32[3,2,3]{2,1,0:T(2,128)} %match.5), custom_call_target="tpu_custom_call", output_to_operand_aliasing={{}: (0, {})} | custom-call | tf_op jit(solution)/shard_map/prep/pallas_call | solution.py:559
  30.3 1.1 %collective-permute-done.3.got_o = f32[9,16,128]{2,1,0:T(8,128)S(1)} collective-permute-done((f32[9,16,128]{2,1,0:T(8,128)S(1)}, f32[9,16,128]{2,1,0:T(8,128)S(1)}, u32[]{:S(2)}, u32[]{:S(2)}) %collective-permute-start.3) | collective-permute-done | bytes 73760 | tf_op jit(solution)/shard_map/ppermute | solution.py:514
  31.3 0.0 collective-permute-done.2.second
  31.3 0.0 collective-permute-done.1.third
  31.3 0.1 join.1.w_mine
  31.4 3.9 %collective-permute-start.4 = (f32[8,128]{1,0:T(8,128)S(1)}, f32[8,128]{1,0:T(8,128)S(1)}, u32[]{:S(2)}, u32[]{:S(2)}) collective-permute-start(f32[8,128]{1,0:T(8,128)S(1)} %join.1.w_mine), channel_id=1, source_target_pairs={{0,1},{1,0},{2,3},{3,2},{4,5},{5,4},{6,7},{7,6},{8,9},{9,8},{10,11... | collective-permute-start | bytes 12296 | tf_op jit(solution)/shard_map/ppermute | solution.py:514
  35.3 0.8 %collective-permute-done.4.w_theirs = f32[8,128]{1,0:T(8,128)S(1)} collective-permute-done((f32[8,128]{1,0:T(8,128)S(1)}, f32[8,128]{1,0:T(8,128)S(1)}, u32[]{:S(2)}, u32[]{:S(2)}) %collective-permute-start.4) | collective-permute-done | bytes 4128 | tf_op jit(solution)/shard_map/ppermute | solution.py:514
  36.1 5.9 %transport.1 = (f32[3,4,40,1024]{3,2,1,0:T(8,128)}, f32[3,40,1024]{2,1,0:T(8,128)}, f32[3,17,8,56,128]{4,3,2,1,0:T(8,128)S(1)}) custom-call(f32[3,17,8,56,128]{4,3,2,1,0:T(8,128)S(1)} %prep.1._, f32[8,128]{1,0:T(8,128)S(1)} %join.1.w_mine, f32[8,128]{1,0:T(8,128)S(1)} %collective-permute-done.4.w_theirs, ...), custom_call_target="tpu_custom_call", output_to_operand_aliasing={{2}: (0, {})} | custom-call | tf_op jit(solution)/shard_map/transport/pallas_call | solution.py:581
  (2 shorter events, 0.0 us)
Async XLA Ops:
  3.2 9.7 %collective-permute-start = (f32[9,16,128]{2,1,0:T(8,128)S(1)}, f32[9,16,128]{2,1,0:T(8,128)S(1)}, u32[]{:S(2)}, u32[]{:S(2)}) collective-permute-start(f32[9,16,128]{2,1,0:T(8,128)S(1)} %get-tuple-element.10), channel_id=1, source_target_pairs={{0,1},{1,0},{2,3},{3,2},{4,5},{5,4},{6,7},{7,6},{8,9},{9,8},{10,11... | collective-permute-start | bytes 221192 | tf_op jit(solution)/shard_map/ppermute | solution.py:514
  12.9 18.4 %collective-permute-start.2 = (f32[152,128]{1,0:T(8,128)S(1)}, f32[152,128]{1,0:T(8,128)S(1)}, u32[]{:S(2)}, u32[]{:S(2)}) collective-permute-start(f32[152,128]{1,0:T(8,128)S(1)} %chip.1), channel_id=1, source_target_pairs={{508,0},{5,1},{510,2},{7,3},{0,4},{9,5},{2,6},{11,7},{4,8},{13,9},... | collective-permute-start | bytes 233480 | tf_op jit(solution)/shard_map/ppermute | solution.py:514
  23.3 8.0 %collective-permute-start.1 = (f32[152,128]{1,0:T(8,128)S(1)}, f32[152,128]{1,0:T(8,128)S(1)}, u32[]{:S(2)}, u32[]{:S(2)}) collective-permute-start(f32[152,128]{1,0:T(8,128)S(1)} %chip.1), channel_id=1, source_target_pairs={{506,0},{7,1},{508,2},{9,3},{510,4},{11,5},{0,6},{13,7},{2,8},{15,... | collective-permute-start | bytes 233480 | tf_op jit(solution)/shard_map/ppermute | solution.py:514
  25.2 6.1 %collective-permute-start.3 = (f32[9,16,128]{2,1,0:T(8,128)S(1)}, f32[9,16,128]{2,1,0:T(8,128)S(1)}, u32[]{:S(2)}, u32[]{:S(2)}) collective-permute-start(f32[9,16,128]{2,1,0:T(8,128)S(1)} %stamp.1), channel_id=1, source_target_pairs={{0,511},{1,2},{2,1},{3,4},{4,3},{5,6},{6,5},{7,8},{8,7},{9,10},{10... | collective-permute-start | bytes 221192 | tf_op jit(solution)/shard_map/ppermute | solution.py:514
  31.4 4.7 %collective-permute-start.4 = (f32[8,128]{1,0:T(8,128)S(1)}, f32[8,128]{1,0:T(8,128)S(1)}, u32[]{:S(2)}, u32[]{:S(2)}) collective-permute-start(f32[8,128]{1,0:T(8,128)S(1)} %join.1.w_mine), channel_id=1, source_target_pairs={{0,1},{1,0},{2,3},{3,2},{4,5},{5,4},{6,7},{7,6},{8,9},{9,8},{10,11... | collective-permute-start | bytes 12296 | tf_op jit(solution)/shard_map/ppermute | solution.py:514
